TPU v7x, 512 devices: a whole 4x8x8 slice. The times are simulated.
512 devices in a mesh: dp: 16 (over z, core), seq: 32 (over x, y).
Axes of the slice: x: 4, y: 8, z: 8, core: 2. Of those that a mesh axis runs over, the one named last changes fastest.
Arguments:
- inputs: bfloat16 [16, 4096, 4096], P('dp', 'seq'), may hold values from -6 to 6
- out_grads: bfloat16 [16, 4096, 14336], P('dp', 'seq'), may hold values from -6 to 6
- valid: int32 [16, 4096], P('dp', 'seq'), may hold values 0 or 1
- doc_blocks: int32 [16, 4], P('dp'), may hold values from 1 to 16, 32 in all within a row
- doc_ids: int32 [64], replicated, may hold values from 0 to 63, each once
- proj_in: bfloat16 [4096, 64], P('seq'), may hold values from -0.09375 to 0.09375
- proj_out: bfloat16 [14336, 64], P('seq'), may hold values from -0.046875 to 0.046875
- test_grads: bfloat16 [1024, 4096], P('seq'), may hold values from -192 to 192
Outputs:
- scores: float32 [64, 1024], P(None, 'seq')
Inputs may be any that keep to these rules, and one draw needn't show every extreme that they name: `doc_blocks`: each group's lengths sum to 32; the largest is 16 in every group. `doc_ids`: every document number appears once.
All inputs are finite; a program needn't handle non-finite values. No bound on the sum of `valid` on one device may be relied on, other than what follows from the above.
Results may differ from a plain program's by a relative error of at most 0.0003.
Values may be sent and summed in bfloat16 or wider, within the bound.
A program may use at most 64 MiB of HBM per device.

v0:
```python
import jax
import jax.numpy as jnp
from jax import lax
from jax.sharding import PartitionSpec as P

PROJ_OUT = 64
FEAT = 4096
BLOCK = 128
DOC_GRP = 4


def per_device(inputs, out_grads, valid, doc_blocks, doc_ids, proj_in, proj_out, test_grads):
    tokens = inputs[0]
    outgrad = out_grads[0]
    slots = tokens.shape[0]
    columns = tokens
    px = jnp.dot(
        columns,
        lax.all_gather(proj_in, "seq", axis=0, tiled=True),
        preferred_element_type=jnp.float32,
    )
    columns = outgrad
    pg = jnp.dot(
        columns,
        lax.all_gather(proj_out, "seq", axis=0, tiled=True),
        preferred_element_type=jnp.float32,
    )
    ends = jnp.cumsum(doc_blocks[0])
    position = lax.axis_index("seq") * slots + jnp.arange(slots, dtype=jnp.int32)
    blk = position // BLOCK
    owner = jnp.sum((blk[:, None] >= ends[None, :]).astype(jnp.int32), axis=1)
    onehot = (
        (owner[:, None] == jnp.arange(DOC_GRP, dtype=jnp.int32)[None, :]) & (valid[0][:, None] == 1)
    ).astype(jnp.float32)
    weighted = (onehot[:, :, None] * pg[:, None, :]).reshape(slots, DOC_GRP * PROJ_OUT)
    partial_grads = jnp.dot(weighted.T, px, precision=lax.Precision.HIGHEST).reshape(DOC_GRP, FEAT)
    ndocs = DOC_GRP * lax.axis_size("dp")
    group_grads = lax.psum(partial_grads, "seq")
    doc_grads = lax.all_gather(group_grads, "dp", axis=0, tiled=True)
    gram = jnp.dot(doc_grads, doc_grads.T, precision=lax.Precision.HIGHEST)
    cross = jnp.dot(doc_grads, test_grads.astype(jnp.float32).T, precision=lax.Precision.HIGHEST)
    damp = 0.1 * jnp.trace(gram) / ndocs
    matrix = gram / ndocs + damp * jnp.eye(ndocs, dtype=jnp.float32)
    factor = jnp.linalg.cholesky(matrix)
    middle = lax.linalg.triangular_solve(factor, cross, left_side=True, lower=True)
    solved = lax.linalg.triangular_solve(
        factor, middle, left_side=True, lower=True, transpose_a=True
    )
    placing = (doc_ids[None, :] == jnp.arange(ndocs, dtype=jnp.int32)[:, None]).astype(jnp.float32)
    return jnp.dot(placing, solved, precision=lax.Precision.HIGHEST)


def solution(mesh):
    in_specs = (
        P("dp", "seq", None),
        P("dp", "seq", None),
        P("dp", "seq"),
        P("dp", None),
        P(),
        P("seq", None),
        P("seq", None),
        P("seq", None),
    )
    out_specs = P(None, "seq")
    return jax.shard_map(
        per_device, mesh=mesh, in_specs=in_specs, out_specs=out_specs, check_vma=False
    )
```

profile of v0, /device:TPU:1, one launch (start us, length us, event | category | flops | bytes accessed | tf_op | source)
XLA Modules:
  0.0 325.9 jit_solution(14330074124522014039)
XLA Ops:
  6.5 0.0 copy-start
  6.5 0.0 all-gather.5.cloned.1.call-start
  6.5 0.7 all-gather.5.cloned.1.call-update
  7.3 0.0 all-reduce.2.cloned.1.call-start
  7.3 0.8 reduce-window.8
  8.1 0.1 convert_reduce_fusion
  8.2 41.4 %all_gather.10 = bf16[4096,64]{0,1:T(8,128)(2,1)S(1)} all-gather(bf16[128,64]{0,1:T(8,128)(2,1)} %param.13), channel_id=1, replica_groups=mesh['dp'=16,'seq'=32] {'seq'}, dimensions={0}, use_global_device_ids=true | all-gather | bytes 540672 | tf_op jit(solution)/shard_map/all_gather | solution.py:19
  49.6 0.7 compare_bitcast_fusion
  50.3 0.0 copy-done
  50.3 0.5 fusion.2
  50.8 44.7 %all-gather.5.cloned.1.call-done = bf16[32,448,64]{1,2,0:T(8,128)(2,1)} async-done(((bf16[1,448,64]{1,2,0:T(8,128)(2,1)}), bf16[32,448,64]{1,2,0:T(8,128)(2,1)}) %all-gather.5.cloned.1.call-update) | async-done | bytes 1835024 | tf_op jit(solution)/shard_map/all_gather | solution.py:25
  95.6 2.8 copy.20
  98.3 3.4 %reshape.113 = bf16[14336,64]{0,1:T(8,128)(2,1)} reshape(bf16[32,448,64]{1,0,2:T(8,128)(2,1)S(1)} %copy.20) | data formatting | bytes 3670016
  101.7 4.0 %fusion = f32[128,64]{0,1:T(8,128)S(1)} fusion(bf16[14336,64]{0,1:T(8,128)(2,1)} %reshape.113, bf16[1,128,14336]{2,1,0:T(8,128)(2,1)} %param.9), kind=kOutput, calls=%fused_computation | convolution fusion | flops 234881024 | bytes 5537792 | tf_op jit(solution)/shard_map/dot_general | solution.py:23
  105.7 0.3 fusion.15
  106.0 0.7 reshape.111
  106.7 0.0 all-reduce.2.cloned.1.call-update
  106.7 0.0 all-gather.7.cloned.1.call-start
  106.8 147.6 %all-reduce.2.cloned.1.call-done = f32[4,4096]{1,0:T(4,128)} async-done(((f32[4,4096]{1,0:T(4,128)}), f32[4,4096]{1,0:T(4,128)}) %all-reduce.2.cloned.1.call-update) | async-done | bytes 65552 | tf_op jit(solution)/shard_map/psum | solution.py:38
  254.4 0.0 all-gather.7.cloned.1.call-update
  254.4 0.0 copy-start.1
  254.4 47.1 %all-gather.7.cloned.1.call-done = f32[16,4,4096]{2,1,0:T(4,128)} async-done(((f32[1,4,4096]{2,1,0:T(4,128)}), f32[16,4,4096]{2,1,0:T(4,128)}) %all-gather.7.cloned.1.call-update) | async-done | bytes 1048592 | tf_op jit(solution)/shard_map/all_gather | solution.py:39
  301.5 1.6 reshape.115
  303.1 0.0 copy-start.2
  303.1 1.6 select_reduce_fusion.1
  304.7 0.1 copy.22
  304.8 0.1 copy.23
  305.6 5.8 %cholesky.17 = f32[64,64]{1,0:T(8,128)S(1)} custom-call(f32[64,64]{1,0:T(8,128)S(1)} %fusion.10), custom_call_target="Cholesky" | custom-call | tf_op jit(solution)/shard_map/jit(cholesky)/cholesky | solution.py:44
  311.4 0.6 compare_reduce_fusion
  312.1 0.7 fusion.4
  312.8 4.9 %custom-call.8 = f32[1,64,64]{1,2,0:T(8,128)S(1)} custom-call(f32[1,64,64]{2,1,0:T(8,128)S(1)} %fusion.4), custom_call_target="InvertDiagBlocksLowerTriangular" | custom-call | tf_op jit(solution)/shard_map/triangular_solve | solution.py:46
  317.6 0.0 copy-done.1
  317.7 0.6 fusion.16
  318.3 0.1 fusion.7
  318.4 0.2 fusion.5
  318.6 0.0 copy-done.2
  318.6 0.8 fusion.11
  (6 shorter events, 0.1 us)
Async XLA Ops:
  6.5 43.8 %copy-start = (bf16[1,128,4096]{2,1,0:T(8,128)(2,1)S(1)}, bf16[1,128,4096]{2,1,0:T(8,128)(2,1)}, u32[]{:S(2)}) copy-start(bf16[1,128,4096]{2,1,0:T(8,128)(2,1)} %param.8) | copy-start | bytes 3145732
  6.5 89.0 %all-gather.5.cloned.1.call-start = ((), (), s32[]{:S(2)}) async-start(), calls=%async_computation.1 | async-start | bytes 2162688 | tf_op jit(solution)/shard_map/all_gather | solution.py:25
  7.3 247.2 %all-reduce.2.cloned.1.call-start = ((), (), s32[]{:S(2)}) async-start(), calls=%async_computation | async-start | bytes 131072 | tf_op jit(solution)/shard_map/psum | solution.py:38
  106.7 194.8 %all-gather.7.cloned.1.call-start = ((), (), s32[]{:S(2)}) async-start(), calls=%async_computation.2 | async-start | bytes 1114112 | tf_op jit(solution)/shard_map/all_gather | solution.py:39
  254.4 63.2 %copy-start.1 = (bf16[32,4096]{1,0:T(8,128)(2,1)S(1)}, bf16[32,4096]{1,0:T(8,128)(2,1)}, u32[]{:S(2)}) copy-start(bf16[32,4096]{1,0:T(8,128)(2,1)} %param.15) | copy-start | bytes 786436
  303.1 15.5 %copy-start.2 = (s32[64]{0:T(128)S(1)}, s32[64]{0:T(128)}, u32[]{:S(2)}) copy-start(s32[64]{0:T(128)} %param.12) | copy-start | bytes 772
Sparse Core Ops, SparseCore 0:
  10.5 84.9 all-gather.4
  106.8 147.5 all-reduce.1
  256.5 44.9 all-gather.6
where the time goes:
time: 326 us
  waiting for transfers between devices  240 us (74%)
  blocking collectives  41.4 us (13%)
  between operations  13.9 us (4%)
  other arithmetic  13.7 us (4%)
  local copies, waits for them, and re-layouts  8.61 us (3%)
  matrix products  8 us (2%)
    psum x1, waiting for transfers between devices, per_device(): group_grads = lax.psum(partial_grads, 'seq')  148 us
    all_gather x1, waiting for transfers between devices, per_device(): doc_grads = lax.all_gather(group_grads, 'dp', axis=0, tiled=True)  47.1 us
    all_gather x1, waiting for transfers between devices, per_device(): lax.all_gather(proj_out, 'seq', axis=0, tiled=True)  44.7 us
    all_gather x1, blocking collectives, per_device(): lax.all_gather(proj_in, 'seq', axis=0, tiled=True)  41.4 us
  transfers between devices with their start and end apart: 3, of which 3 were waited for; matrix products, arithmetic and copies ran while one was open for 1% of the time, Pallas kernels for 0%

commit v1 on v0

v1 whole, which is shorter than its diff:
```python
import jax
import jax.numpy as jnp
from jax import lax
from jax.experimental import pallas as pl
from jax.experimental.pallas import tpu as pltpu
from jax.sharding import PartitionSpec as P

MESH = pl.DeviceIdType.MESH
F32 = jnp.float32
BF16 = jnp.bfloat16
HIGH = lax.Precision.HIGHEST
NX, NY, NZ = 4, 8, 8
NSEQ, NDP = NX * NY, 2 * NZ
KO, KP, KI = 448, 512, 128
NDOCS = 64
NT = (((1,), (1,)), ((), ()))
Y_ORDER = (1, 7, 2, 6, 3, 5, 4)
X_ORDER = (1, 3, 2)


def kernel(
    in_hbm, og_hbm, valid_ref, blocks_ref, pin_ref, pout_ref, test_ref, out_ref,
    tok, grad, wo, wi, pad, send_b, recv_b, send_c, recv_c, recv_c2, send_d, recv_d, send_e, recv_e,
    load_sem, so, si, sdo, sdi, ro, ri, rso, rsi, rgo, rgi, phase_send, phase_recv,
):
    dp = lax.axis_index("dp")
    seq = lax.axis_index("seq")
    core = lax.rem(dp, 2)
    sibling = (dp + 1 - 2 * core, seq)
    x, y = seq // NY, lax.rem(seq, NY)

    def shard(i, j):
        return lax.rem(x + i, NX) * NY + lax.rem(y + j, NY)

    load_tok = pltpu.make_async_copy(in_hbm, tok, load_sem.at[0])
    load_grad = pltpu.make_async_copy(og_hbm, grad, load_sem.at[1])
    load_tok.start()
    load_grad.start()

    barrier = pltpu.get_barrier_semaphore()

    def greet_seq(i, carry):
        pl.semaphore_signal(
            barrier, inc=1, device_id=(dp, lax.rem(seq + i, NSEQ)), device_id_type=MESH
        )
        return carry

    def greet_dp(i, carry):
        pl.semaphore_signal(
            barrier, inc=1, device_id=(lax.rem(dp + i, NDP), seq), device_id_type=MESH
        )
        return carry

    lax.fori_loop(1, NSEQ, greet_seq, 0)
    lax.fori_loop(1, NDP, greet_dp, 0)

    row = lax.broadcasted_iota(jnp.int32, (64, 64), 0)
    col = lax.broadcasted_iota(jnp.int32, (64, 64), 1)
    source = jnp.where(row < 32, 2 * row, 2 * row - 63)
    order = jnp.where(col == source, 1.0, 0.0).astype(BF16)
    pad[...] = jnp.zeros_like(pad)
    pad[:, 0:KO] = jnp.dot(order, pout_ref[...], preferred_element_type=F32)
    left = pad[...]
    right = pltpu.roll(left, KP - KO, 1)
    odd = lax.rem(seq, 2)
    own_out = jnp.where(odd == 1, right, left).astype(BF16)
    wo[seq, 0] = own_out[0:32]
    wo[seq, 1] = own_out[32:64]
    wi[seq, 0] = pin_ref[0:32, :]
    wi[seq, 1] = pin_ref[32:64, :]

    pl.semaphore_wait(barrier, NSEQ - 1 + NDP - 1)

    def send_out(k, i, j):
        pltpu.make_async_remote_copy(
            wo.at[k, core], wo.at[k, core], so, ro.at[k],
            device_id=(dp, shard(i, j)), device_id_type=MESH,
        ).start()

    def send_in(k, i, j):
        pltpu.make_async_remote_copy(
            wi.at[k, core], wi.at[k, core], si, ri.at[k],
            device_id=(dp, shard(i, j)), device_id_type=MESH,
        ).start()

    def recv_out(k):
        pltpu.make_async_remote_copy(
            wo.at[k, core], wo.at[k, core], so, ro.at[k], device_id=sibling, device_id_type=MESH
        ).wait_recv()

    def recv_in(k):
        pltpu.make_async_remote_copy(
            wi.at[k, core], wi.at[k, core], si, ri.at[k], device_id=sibling, device_id_type=MESH
        ).wait_recv()

    for i in X_ORDER:
        send_in(seq, i, 0)
    for j in Y_ORDER:
        send_out(seq, 0, j)
    for i in X_ORDER:
        send_out(seq, i, 0)
    for j in Y_ORDER:
        send_in(seq, 0, j)

    def forward_in(i):
        k = shard(i, 0)
        recv_in(k)
        for j in Y_ORDER:
            send_in(k, 0, j)

    def forward_out(j):
        k = shard(0, j)
        recv_out(k)
        for i in X_ORDER:
            send_out(k, i, 0)
        pltpu.make_async_remote_copy(
            wo.at[k, core], wo.at[k, core], sdo, rso.at[k], device_id=sibling, device_id_type=MESH
        ).start()

    forward_in(1)
    forward_in(3)
    forward_out(1)
    forward_out(7)
    forward_in(2)
    for j in (2, 6, 3, 5, 4):
        forward_out(j)

    for j in Y_ORDER:
        k = shard(0, j)
        recv_in(k)
        pltpu.make_async_remote_copy(
            wi.at[k, core], wi.at[k, core], sdi, rsi.at[k], device_id=sibling, device_id_type=MESH
        ).start()

    load_tok.wait()
    load_grad.wait()

    def product(group):
        first = pl.multiple_of(group * NY, NY)
        lane = lax.broadcasted_iota(jnp.int32, (64, 128), 1)
        parts = []
        for q in range(NY // 2):
            even = wo[first + 2 * q].reshape(64, KP)
            odds = wo[first + 2 * q + 1].reshape(64, KP)
            joint = jnp.where(lane < 64, even[:, 384:512].astype(F32), odds[:, 0:128].astype(F32))
            parts += [even[:, 0:384], joint.astype(BF16), odds[:, 128:512]]
        weights = jnp.concatenate(parts, axis=1)
        columns = pl.ds(pl.multiple_of(group * NY * KO, NY * KO), NY * KO)
        pg = lax.dot_general(weights, grad[:, columns], NT, preferred_element_type=F32)
        weights = jnp.concatenate([wi[first + q].reshape(64, KI) for q in range(NY)], axis=1)
        columns = pl.ds(pl.multiple_of(group * NY * KI, NY * KI), NY * KI)
        px = lax.dot_general(weights, tok[:, columns], NT, preferred_element_type=F32)
        return pg, px

    def gather_sibling_row():
        for j in Y_ORDER:
            k = shard(0, j)
            pltpu.make_async_remote_copy(
                wo.at[k, core], wo.at[k, 1 - core], sdo, rso.at[k],
                device_id=sibling, device_id_type=MESH,
            ).wait_recv()
            pltpu.make_async_remote_copy(
                wi.at[k, core], wi.at[k, 1 - core], sdi, rsi.at[k],
                device_id=sibling, device_id_type=MESH,
            ).wait_recv()

    def exchange_group(i):
        group = lax.rem(x + i, NX)
        for j in (0,) + Y_ORDER:
            recv_out(shard(i, j))
        for j in Y_ORDER:
            recv_in(shard(i, j))
        rows = pl.ds(pl.multiple_of(group * NY, NY), NY)
        pltpu.make_async_remote_copy(
            wo.at[rows, core], wo.at[rows, core], sdo, rgo.at[i - 1],
            device_id=sibling, device_id_type=MESH,
        ).start()
        pltpu.make_async_remote_copy(
            wi.at[rows, core], wi.at[rows, core], sdi, rgi.at[i - 1],
            device_id=sibling, device_id_type=MESH,
        ).start()

    def await_group(i):
        group = lax.rem(x + i, NX)
        rows = pl.ds(pl.multiple_of(group * NY, NY), NY)
        pltpu.make_async_remote_copy(
            wo.at[rows, core], wo.at[rows, 1 - core], sdo, rgo.at[i - 1],
            device_id=sibling, device_id_type=MESH,
        ).wait_recv()
        pltpu.make_async_remote_copy(
            wi.at[rows, core], wi.at[rows, 1 - core], sdi, rgi.at[i - 1],
            device_id=sibling, device_id_type=MESH,
        ).wait_recv()
        return group

    gather_sibling_row()
    pg, px = product(x)
    exchange_group(1)
    exchange_group(3)
    more_g, more_x = product(await_group(1))
    pg, px = pg + more_g, px + more_x
    more_g, more_x = product(await_group(3))
    pg, px = pg + more_g, px + more_x
    exchange_group(2)
    more_g, more_x = product(await_group(2))
    pg, px = pg + more_g, px + more_x

    pg = jnp.where(valid_ref[...] == 1, pg, 0.0)
    block_grad = lax.dot_general(pg, px, NT, precision=HIGH, preferred_element_type=F32)
    folded = jnp.concatenate([block_grad[0:32], block_grad[32:64]], axis=1)
    send_b[...] = folded.reshape(NSEQ, 1, 128)

    def seq_copy(phase, src, dst, i):
        return pltpu.make_async_remote_copy(
            src, dst, phase_send.at[phase], phase_recv.at[phase],
            device_id=(dp, lax.rem(seq + i, NSEQ)), device_id_type=MESH,
        )

    def dp_copy(phase, src, dst, i):
        return pltpu.make_async_remote_copy(
            src, dst, phase_send.at[phase], phase_recv.at[phase],
            device_id=(lax.rem(dp + i, NDP), seq), device_id_type=MESH,
        )

    def scatter(i, carry):
        seq_copy(0, send_b.at[lax.rem(seq + i, NSEQ)], recv_b.at[seq], i).start()
        return carry

    lax.fori_loop(1, NSEQ, scatter, 0)
    recv_b[seq] = send_b[seq]
    block = lax.broadcasted_iota(jnp.int32, (8, NSEQ), 1)
    doc = lax.broadcasted_iota(jnp.int32, (8, NSEQ), 0)
    owner = jnp.zeros((8, NSEQ), jnp.int32)
    end = 0
    for j in range(4):
        end = end + blocks_ref[0, j]
        owner = owner + jnp.where(block >= end, 1, 0)
    member = jnp.where(owner == doc, 1.0, 0.0)
    seq_copy(0, recv_b.at[pl.ds(0, NSEQ - 1)], recv_b.at[pl.ds(0, NSEQ - 1)], 1).wait_recv()
    blocks = recv_b[...].reshape(NSEQ, 128)
    docs = jnp.dot(member, blocks, precision=HIGH, preferred_element_type=F32)
    send_c[...] = docs[0:4]

    def gather_dp(i, carry):
        dp_copy(1, send_c, recv_c.at[dp], i).start()
        return carry

    def gather_seq(i, carry):
        seq_copy(2, send_c, recv_c2.at[seq], i).start()
        return carry

    lax.fori_loop(1, NDP, gather_dp, 0)
    lax.fori_loop(1, NSEQ, gather_seq, 0)
    recv_c[dp] = docs[0:4]
    recv_c2[seq] = docs[0:4]

    dp_copy(1, recv_c.at[pl.ds(0, NDP - 1)], recv_c.at[pl.ds(0, NDP - 1)], 1).wait_recv()
    every = recv_c[...].reshape(NDOCS, 128)
    partial = lax.dot_general(docs, every, NT, precision=HIGH, preferred_element_type=F32)
    send_d[...] = partial[0:4]

    def reduce_seq(i, carry):
        seq_copy(3, send_d, recv_d.at[seq], i).start()
        return carry

    lax.fori_loop(1, NSEQ, reduce_seq, 0)
    recv_d[seq] = partial[0:4]

    seq_copy(2, recv_c2.at[pl.ds(0, NSEQ - 1)], recv_c2.at[pl.ds(0, NSEQ - 1)], 1).wait_recv()
    own = jnp.concatenate([recv_c2[t] for t in range(NSEQ)], axis=1)
    high = own.astype(BF16)
    rest = own - high.astype(F32)
    middle = rest.astype(BF16)
    low = (rest - middle.astype(F32)).astype(BF16)
    test = test_ref[...]
    cross = lax.dot_general(high, test, NT, preferred_element_type=F32)
    cross = cross + (
        lax.dot_general(middle, test, NT, preferred_element_type=F32)
        + lax.dot_general(low, test, NT, preferred_element_type=F32)
    )

    seq_copy(3, recv_d.at[pl.ds(0, NSEQ - 1)], recv_d.at[pl.ds(0, NSEQ - 1)], 1).wait_recv()
    gram_rows = jnp.sum(recv_d[...], axis=0)
    send_e[...] = jnp.zeros_like(send_e)
    send_e[:, 0:64] = gram_rows
    send_e[:, 64:96] = cross

    def gather_rows(i, carry):
        dp_copy(4, send_e, recv_e.at[dp], i).start()
        return carry

    lax.fori_loop(1, NDP, gather_rows, 0)
    recv_e[dp] = send_e[...]
    dp_copy(4, recv_e.at[pl.ds(0, NDP - 1)], recv_e.at[pl.ds(0, NDP - 1)], 1).wait_recv()
    out_ref[...] = recv_e[...].reshape(NDOCS, 128)

    for sem, buf in ((so, wo), (sdo, wo), (si, wi), (sdi, wi)):
        part = buf.at[pl.ds(0, NSEQ - 1), 0]
        pltpu.make_async_remote_copy(
            part, part, sem, ro.at[0], device_id=sibling, device_id_type=MESH
        ).wait_send()
    seq_copy(0, send_b.at[pl.ds(0, NSEQ - 1)], send_b.at[pl.ds(0, NSEQ - 1)], 1).wait_send()
    dp_copy(1, recv_c.at[pl.ds(0, NDP - 1)], recv_c.at[pl.ds(0, NDP - 1)], 1).wait_send()
    seq_copy(2, recv_c2.at[pl.ds(0, NSEQ - 1)], recv_c2.at[pl.ds(0, NSEQ - 1)], 1).wait_send()
    seq_copy(3, recv_d.at[pl.ds(0, NSEQ - 1)], recv_d.at[pl.ds(0, NSEQ - 1)], 1).wait_send()
    dp_copy(4, recv_e.at[pl.ds(0, NDP - 1)], recv_e.at[pl.ds(0, NDP - 1)], 1).wait_send()


def exchange(tokens, outgrad, valid, doc_blocks, proj_in, proj_out, test_grads):
    vmem = pl.BlockSpec(memory_space=pltpu.VMEM)
    anywhere = pl.BlockSpec(memory_space=pl.ANY)
    dma = pltpu.SemaphoreType.DMA
    return pl.pallas_call(
        kernel,
        name="attribution",
        out_shape=jax.ShapeDtypeStruct((NDOCS, 128), F32),
        in_specs=[
            anywhere, anywhere, vmem, pl.BlockSpec(memory_space=pltpu.SMEM), vmem, vmem, vmem,
        ],
        out_specs=vmem,
        scratch_shapes=[
            pltpu.VMEM((128, 4096), BF16),
            pltpu.VMEM((128, 14336), BF16),
            pltpu.VMEM((NSEQ, 2, 32, KP), BF16),
            pltpu.VMEM((NSEQ, 2, 32, KI), BF16),
            pltpu.VMEM((64, KP), F32),
            pltpu.VMEM((NSEQ, 1, 128), F32),
            pltpu.VMEM((NSEQ, 1, 128), F32),
            pltpu.VMEM((4, 128), F32),
            pltpu.VMEM((NDP, 4, 128), F32),
            pltpu.VMEM((NSEQ, 4, 128), F32),
            pltpu.VMEM((4, 64), F32),
            pltpu.VMEM((NSEQ, 4, 64), F32),
            pltpu.VMEM((4, 128), F32),
            pltpu.VMEM((NDP, 4, 128), F32),
            dma((2,)),
            dma, dma, dma, dma,
            dma((NSEQ,)), dma((NSEQ,)), dma((NSEQ,)), dma((NSEQ,)),
            dma((NX - 1,)), dma((NX - 1,)),
            dma((5,)), dma((5,)),
        ],
        compiler_params=pltpu.CompilerParams(
            collective_id=0, has_side_effects=True, vmem_limit_bytes=40 << 20
        ),
    )(tokens, outgrad, valid, doc_blocks, proj_in.T, proj_out.T, test_grads)


def per_device(inputs, out_grads, valid, doc_blocks, doc_ids, proj_in, proj_out, test_grads):
    both = exchange(inputs[0], out_grads[0], valid, doc_blocks, proj_in, proj_out, test_grads)
    gram, cross = both[:, 0:64], both[:, 64:96]
    damp = 0.1 * jnp.trace(gram) / NDOCS
    matrix = gram / NDOCS + damp * jnp.eye(NDOCS, dtype=F32)
    factor = jnp.linalg.cholesky(matrix)
    middle = lax.linalg.triangular_solve(factor, cross, left_side=True, lower=True)
    solved = lax.linalg.triangular_solve(
        factor, middle, left_side=True, lower=True, transpose_a=True
    )
    placing = (doc_ids[None, :] == jnp.arange(NDOCS, dtype=jnp.int32)[:, None]).astype(F32)
    return jnp.dot(placing, solved, precision=HIGH)


def solution(mesh):
    in_specs = (
        P("dp", "seq", None),
        P("dp", "seq", None),
        P("dp", "seq"),
        P("dp", None),
        P(),
        P("seq", None),
        P("seq", None),
        P("seq", None),
    )
    return jax.shard_map(
        per_device, mesh=mesh, in_specs=in_specs, out_specs=P(None, "seq"), check_vma=False
    )
```

time: 326 us -> 81.2 us (0.25)
  waiting for transfers between devices: 240 us -> 0 us
  Pallas kernels: 0 us -> 59 us
  blocking collectives: 41.4 us -> 0 us
  between operations: 13.9 us -> 0.72 us
  matrix products: 8 us -> 1.25 us
    psum x1 -> x0, waiting for transfers between devices: 148 us -> none  [per_device(): group_grads = lax.psum(partial_grads, 'seq')]
    all_gather x2 -> x0, waiting for transfers between devices: 91.8 us -> none  [the longest x1 47.1 us: per_device(): doc_grads = lax.all_gather(group_grads, 'dp', axis=0, tiled=True)]
    pallas_call x0 -> x1, Pallas kernels: none -> 59 us  [exchange(): pl.pallas_call(kernel, name='attribution', out_shape=jax.ShapeDtypeStruct...]
    all_gather x1 -> x0, blocking collectives: 41.4 us -> none  [per_device(): lax.all_gather(proj_in, 'seq', axis=0, tiled=True)]
    dot_general x6 -> x1, matrix products: 7.69 us -> 0.82 us  [per_device(): return jnp.dot(placing, solved, precision=HIGH)]
    unnamed x8 -> x16, local copies, waits for them, and re-layouts: 4.99 us -> 7.09 us
  transfers between devices with their start and end apart: 3 -> 0, of which waited for: 3 -> 0; matrix products, arithmetic and copies ran while one was open for 1% -> 0% of each run, Pallas kernels for 0% -> 0%
where the time goes in v1:
time: 81.2 us; the launch traced here: 80.9 us
  Pallas kernels  59 us (73%)
  other arithmetic  12.7 us (16%)
  local copies, waits for them, and re-layouts  7.17 us (9%)
  matrix products  1.25 us (2%)
    pallas_call x1, Pallas kernels, exchange(): pl.pallas_call(kernel, name='attribution', out_shape=jax.ShapeDtypeStruct...  59 us
    unnamed x16, local copies, waits for them, and re-layouts  7.09 us
    another operation x3, other arithmetic, per_device(): factor = jnp.linalg.cholesky(matrix)  6.52 us
    another operation x2, other arithmetic, per_device(): lax.linalg.triangular_solve(factor, middle, left_side=True, lower=True, t...  5.55 us

profile of v1, /device:TPU:1, one launch (start us, length us, event | category | flops | bytes accessed | tf_op | source)
XLA Modules:
  0.0 80.9 jit_solution(12163021682472944021)
XLA Ops:
  0.0 0.0 copy-start.7
  0.0 0.0 copy-start
  0.0 2.0 %copy-done = bf16[1,128,14336]{2,1,0:T(8,128)(2,1)S(1)} copy-done((bf16[1,128,14336]{2,1,0:T(8,128)(2,1)S(1)}, bf16[1,128,14336]{2,1,0:T(8,128)(2,1)}, u32[]{:S(2)}) %copy-start) | copy-done | bytes 3670040
  2.1 0.0 copy-start.1
  2.1 1.2 %copy-done.1 = bf16[1,128,4096]{2,1,0:T(8,128)(2,1)S(1)} copy-done((bf16[1,128,4096]{2,1,0:T(8,128)(2,1)S(1)}, bf16[1,128,4096]{2,1,0:T(8,128)(2,1)}, u32[]{:S(2)}) %copy-start.1) | copy-done | bytes 1048600
  3.3 0.0 copy-start.2
  3.3 0.9 %copy-done.2 = bf16[32,4096]{1,0:T(8,128)(2,1)S(1)} copy-done((bf16[32,4096]{1,0:T(8,128)(2,1)S(1)}, bf16[32,4096]{1,0:T(8,128)(2,1)}, u32[]{:S(2)}) %copy-start.2) | copy-done | bytes 262168
  4.2 0.0 copy-start.3
  4.2 0.8 %copy-done.3 = bf16[448,64]{0,1:T(8,128)(2,1)S(1)} copy-done((bf16[448,64]{0,1:T(8,128)(2,1)S(1)}, bf16[448,64]{0,1:T(8,128)(2,1)}, u32[]{:S(2)}) %copy-start.3) | copy-done | bytes 57368
  5.1 0.0 copy-start.4
  5.1 0.7 copy-done.4
  5.8 0.0 copy-start.5
  5.8 0.7 copy-done.5
  6.4 0.0 copy-start.6
  6.4 0.7 copy-done.6
  7.1 59.0 %attribution.1 = f32[64,128]{1,0:T(8,128)S(1)} custom-call(bf16[128,4096]{1,0:T(8,128)(2,1)S(1)} %bitcast.18, bf16[128,14336]{1,0:T(8,128)(2,1)S(1)} %bitcast.17, s32[1,128]{1,0:T(1,128)S(1)} %copy-done.5, s32[1,4]{1,0:T(1,128)S(1)} %copy-done.6, bf16[64,128]{1,0:T(8,128)(2,1)S(1)} %bitcast.20, bf16[64,448]{1,0:T(8,128)(2,1)S(1)} %bitcast.19, ...), custom_call_target="tpu_custom_call" | custom-call | tf_op jit(solution)/shard_map/attribution/pallas_call | solution.py:313
  66.1 0.6 select_reduce_fusion.1
  67.4 0.1 copy.9
  67.5 5.8 %cholesky.17 = f32[64,64]{1,0:T(8,128)S(1)} custom-call(f32[64,64]{1,0:T(8,128)S(1)} %fusion.5), custom_call_target="Cholesky" | custom-call | tf_op jit(solution)/shard_map/jit(cholesky)/cholesky | solution.py:353
  73.4 0.6 compare_reduce_fusion
  74.0 0.7 fusion
  74.7 4.9 %custom-call.8 = f32[1,64,64]{1,2,0:T(8,128)S(1)} custom-call(f32[1,64,64]{2,1,0:T(8,128)S(1)} %fusion), custom_call_target="InvertDiagBlocksLowerTriangular" | custom-call | tf_op jit(solution)/shard_map/triangular_solve | solution.py:355
  79.6 0.3 fusion.3
  79.9 0.2 fusion.1
  80.0 0.0 copy-done.7
  80.1 0.8 %fusion.7 = f32[64,32]{0,1:T(8,128)} fusion(f32[64,32]{1,0:T(8,128)S(1)} %fusion.1, s32[64]{0:T(128)S(1)} %copy-done.7), kind=kOutput, calls=%fused_computation.15 | convolution fusion | flops 1576960 | bytes 16640 | tf_op jit(solution)/shard_map/dot_general | solution.py:359
  (3 shorter events, 0.1 us)
Async XLA Ops:
  0.0 80.0 %copy-start.7 = (s32[64]{0:T(128)S(1)}, s32[64]{0:T(128)}, u32[]{:S(2)}) copy-start(s32[64]{0:T(128)} %param.12) | copy-start | bytes 772
  0.0 2.1 %copy-start = (bf16[1,128,14336]{2,1,0:T(8,128)(2,1)S(1)}, bf16[1,128,14336]{2,1,0:T(8,128)(2,1)}, u32[]{:S(2)}) copy-start(bf16[1,128,14336]{2,1,0:T(8,128)(2,1)} %param.9) | copy-start | bytes 11010052
  2.1 1.2 %copy-start.1 = (bf16[1,128,4096]{2,1,0:T(8,128)(2,1)S(1)}, bf16[1,128,4096]{2,1,0:T(8,128)(2,1)}, u32[]{:S(2)}) copy-start(bf16[1,128,4096]{2,1,0:T(8,128)(2,1)} %param.8) | copy-start | bytes 3145732
  3.3 0.9 %copy-start.2 = (bf16[32,4096]{1,0:T(8,128)(2,1)S(1)}, bf16[32,4096]{1,0:T(8,128)(2,1)}, u32[]{:S(2)}) copy-start(bf16[32,4096]{1,0:T(8,128)(2,1)} %test_ref.1) | copy-start | bytes 786436
  4.2 0.8 %copy-start.3 = (bf16[448,64]{0,1:T(8,128)(2,1)S(1)}, bf16[448,64]{0,1:T(8,128)(2,1)}, u32[]{:S(2)}) copy-start(bf16[448,64]{0,1:T(8,128)(2,1)} %param.14) | copy-start | bytes 172036
  5.1 0.7 copy-start.4
  5.8 0.7 copy-start.5
  6.4 0.7 copy-start.6

commit v2 on v1

--- a/solution.py
+++ b/solution.py
@@ -18,9 +18,47 @@
 X_ORDER = (1, 3, 2)
 
 
+def inverse2(p, q, s):
+    scale = 1.0 / (p * s - q * q)
+    return s * scale, -q * scale, p * scale
+
+
+def solve(both, ids):
+    row = lax.broadcasted_iota(jnp.int32, (NDOCS, 128), 0)
+    lane = lax.broadcasted_iota(jnp.int32, (NDOCS, 128), 1)
+    diagonal = jnp.where(row == lane, both, 0.0)
+    trace = jnp.sum(jnp.sum(diagonal, axis=0, keepdims=True), axis=1, keepdims=True)
+    a = jnp.where(lane < NDOCS, both, NDOCS * both) / trace
+    a = a + jnp.where(row == lane, 0.1, 0.0)
+    for k in range(0, NDOCS, 4):
+        r = [a[k + i : k + i + 1, :] for i in range(4)]
+        c = [jnp.broadcast_to(a[:, k + i : k + i + 1], (NDOCS, 128)) for i in range(4)]
+        m = [[c[j][k + i : k + i + 1] for j in range(4)] for i in range(4)]
+        a00, a01, a11 = inverse2(m[0][0], m[1][0], m[1][1])
+        b00, b01, b10, b11 = m[2][0], m[3][0], m[2][1], m[3][1]
+        w00, w01 = a00 * b00 + a01 * b10, a00 * b01 + a01 * b11
+        w10, w11 = a01 * b00 + a11 * b10, a01 * b01 + a11 * b11
+        s00 = m[2][2] - (b00 * w00 + b10 * w10)
+        s01 = m[3][2] - (b00 * w01 + b10 * w11)
+        s11 = m[3][3] - (b01 * w01 + b11 * w11)
+        e00, e01, e11 = inverse2(s00, s01, s11)
+        t2 = r[2] - (w00 * r[0] + w10 * r[1])
+        t3 = r[3] - (w01 * r[0] + w11 * r[1])
+        u2, u3 = e00 * t2 + e01 * t3, e01 * t2 + e11 * t3
+        u0 = a00 * r[0] + a01 * r[1] - (w00 * u2 + w01 * u3)
+        u1 = a01 * r[0] + a11 * r[1] - (w10 * u2 + w11 * u3)
+        rest = a - ((c[0] * u0 + c[1] * u1) + (c[2] * u2 + c[3] * u3))
+        for i, u in enumerate((u0, u1, u2, u3)):
+            rest = jnp.where(row == k + i, u, rest)
+        a = rest
+    number = lax.broadcasted_iota(jnp.int32, (NDOCS, NDOCS), 0)
+    placing = jnp.where(ids == number, 1.0, 0.0)
+    return jnp.dot(placing, a[:, 64:96], precision=HIGH, preferred_element_type=F32)
+
+
 def kernel(
-    in_hbm, og_hbm, valid_ref, blocks_ref, pin_ref, pout_ref, test_ref, out_ref,
-    tok, grad, wo, wi, pad, send_b, recv_b, send_c, recv_c, recv_c2, send_d, recv_d, send_e, recv_e,
+    in_hbm, og_hbm, valid_hbm, blocks_hbm, pin_hbm, pout_hbm, test_hbm, ids_hbm, out_ref,
+    tok, grad, valid_ref, blocks_ref, pin_ref, pout_ref, test_ref, ids_ref, wo, wi, pad, send_b, recv_b, send_c, recv_c, recv_c2, send_d, recv_d, send_e, recv_e,
     load_sem, so, si, sdo, sdi, ro, ri, rso, rsi, rgo, rgi, phase_send, phase_recv,
 ):
     dp = lax.axis_index("dp")
@@ -32,10 +70,21 @@
     def shard(i, j):
         return lax.rem(x + i, NX) * NY + lax.rem(y + j, NY)
 
-    load_tok = pltpu.make_async_copy(in_hbm, tok, load_sem.at[0])
-    load_grad = pltpu.make_async_copy(og_hbm, grad, load_sem.at[1])
-    load_tok.start()
-    load_grad.start()
+    def load(i, src, dst):
+        copy = pltpu.make_async_copy(src, dst, load_sem.at[i])
+        copy.start()
+        return copy
+
+    load_pout = load(0, pout_hbm, pout_ref)
+    load_pin = load(1, pin_hbm, pin_ref)
+    later = [
+        load(2, in_hbm, tok),
+        load(3, og_hbm, grad),
+        load(4, valid_hbm, valid_ref),
+        load(5, blocks_hbm, blocks_ref),
+        load(6, test_hbm, test_ref),
+        load(7, ids_hbm, ids_ref),
+    ]
 
     barrier = pltpu.get_barrier_semaphore()
 
@@ -53,12 +102,30 @@
 
     lax.fori_loop(1, NSEQ, greet_seq, 0)
     lax.fori_loop(1, NDP, greet_dp, 0)
+
+    def finish(last):
+        for sem, buf in ((so, wo), (sdo, wo), (si, wi), (sdi, wi)):
+            part = buf.at[pl.ds(0, NSEQ - 1), 0]
+            pltpu.make_async_remote_copy(
+                part, part, sem, ro.at[0], device_id=sibling, device_id_type=MESH
+            ).wait_send()
+        for phase, buf, count in (
+            (0, send_b, NSEQ), (1, recv_c, NDP), (2, recv_c2, NSEQ), (3, recv_d, NSEQ), (4, recv_e, NDP),
+        ):
+            if phase <= last:
+                part = buf.at[pl.ds(0, count - 1)]
+                pltpu.make_async_remote_copy(
+                    part, part, phase_send.at[phase], phase_recv.at[phase],
+                    device_id=sibling, device_id_type=MESH,
+                ).wait_send()
 
     row = lax.broadcasted_iota(jnp.int32, (64, 64), 0)
     col = lax.broadcasted_iota(jnp.int32, (64, 64), 1)
     source = jnp.where(row < 32, 2 * row, 2 * row - 63)
     order = jnp.where(col == source, 1.0, 0.0).astype(BF16)
     pad[...] = jnp.zeros_like(pad)
+    load_pout.wait()
+    load_pin.wait()
     pad[:, 0:KO] = jnp.dot(order, pout_ref[...], preferred_element_type=F32)
     left = pad[...]
     right = pltpu.roll(left, KP - KO, 1)
@@ -132,8 +199,8 @@
             wi.at[k, core], wi.at[k, core], sdi, rsi.at[k], device_id=sibling, device_id_type=MESH
         ).start()
 
-    load_tok.wait()
-    load_grad.wait()
+    for copy in later:
+        copy.wait()
 
     def product(group):
         first = pl.multiple_of(group * NY, NY)
@@ -292,35 +359,28 @@
     lax.fori_loop(1, NDP, gather_rows, 0)
     recv_e[dp] = send_e[...]
     dp_copy(4, recv_e.at[pl.ds(0, NDP - 1)], recv_e.at[pl.ds(0, NDP - 1)], 1).wait_recv()
-    out_ref[...] = recv_e[...].reshape(NDOCS, 128)
-
-    for sem, buf in ((so, wo), (sdo, wo), (si, wi), (sdi, wi)):
-        part = buf.at[pl.ds(0, NSEQ - 1), 0]
-        pltpu.make_async_remote_copy(
-            part, part, sem, ro.at[0], device_id=sibling, device_id_type=MESH
-        ).wait_send()
-    seq_copy(0, send_b.at[pl.ds(0, NSEQ - 1)], send_b.at[pl.ds(0, NSEQ - 1)], 1).wait_send()
-    dp_copy(1, recv_c.at[pl.ds(0, NDP - 1)], recv_c.at[pl.ds(0, NDP - 1)], 1).wait_send()
-    seq_copy(2, recv_c2.at[pl.ds(0, NSEQ - 1)], recv_c2.at[pl.ds(0, NSEQ - 1)], 1).wait_send()
-    seq_copy(3, recv_d.at[pl.ds(0, NSEQ - 1)], recv_d.at[pl.ds(0, NSEQ - 1)], 1).wait_send()
-    dp_copy(4, recv_e.at[pl.ds(0, NDP - 1)], recv_e.at[pl.ds(0, NDP - 1)], 1).wait_send()
-
-
-def exchange(tokens, outgrad, valid, doc_blocks, proj_in, proj_out, test_grads):
+    out_ref[...] = solve(recv_e[...].reshape(NDOCS, 128), ids_ref[...])
+    finish(4)
+
+
+def exchange(tokens, outgrad, valid, doc_blocks, doc_ids, proj_in, proj_out, test_grads):
     vmem = pl.BlockSpec(memory_space=pltpu.VMEM)
-    anywhere = pl.BlockSpec(memory_space=pl.ANY)
     dma = pltpu.SemaphoreType.DMA
     return pl.pallas_call(
         kernel,
         name="attribution",
-        out_shape=jax.ShapeDtypeStruct((NDOCS, 128), F32),
-        in_specs=[
-            anywhere, anywhere, vmem, pl.BlockSpec(memory_space=pltpu.SMEM), vmem, vmem, vmem,
-        ],
+        out_shape=jax.ShapeDtypeStruct((NDOCS, 32), F32),
+        in_specs=[pl.BlockSpec(memory_space=pltpu.HBM)] * 8,
         out_specs=vmem,
         scratch_shapes=[
             pltpu.VMEM((128, 4096), BF16),
             pltpu.VMEM((128, 14336), BF16),
+            pltpu.VMEM((1, 128), jnp.int32),
+            pltpu.SMEM((1, 4), jnp.int32),
+            pltpu.VMEM((64, KI), BF16),
+            pltpu.VMEM((64, KO), BF16),
+            pltpu.VMEM((32, 4096), BF16),
+            pltpu.VMEM((1, NDOCS), jnp.int32),
             pltpu.VMEM((NSEQ, 2, 32, KP), BF16),
             pltpu.VMEM((NSEQ, 2, 32, KI), BF16),
             pltpu.VMEM((64, KP), F32),
@@ -333,30 +393,22 @@
             pltpu.VMEM((NSEQ, 4, 64), F32),
             pltpu.VMEM((4, 128), F32),
             pltpu.VMEM((NDP, 4, 128), F32),
-            dma((2,)),
+            dma((8,)),
             dma, dma, dma, dma,
             dma((NSEQ,)), dma((NSEQ,)), dma((NSEQ,)), dma((NSEQ,)),
             dma((NX - 1,)), dma((NX - 1,)),
             dma((5,)), dma((5,)),
         ],
         compiler_params=pltpu.CompilerParams(
-            collective_id=0, has_side_effects=True, vmem_limit_bytes=40 << 20
+            collective_id=0, has_side_effects=True, vmem_limit_bytes=60 << 20
         ),
-    )(tokens, outgrad, valid, doc_blocks, proj_in.T, proj_out.T, test_grads)
+    )(tokens, outgrad, valid, doc_blocks, proj_in.T, proj_out.T, test_grads, doc_ids.reshape(1, NDOCS))
 
 
 def per_device(inputs, out_grads, valid, doc_blocks, doc_ids, proj_in, proj_out, test_grads):
-    both = exchange(inputs[0], out_grads[0], valid, doc_blocks, proj_in, proj_out, test_grads)
-    gram, cross = both[:, 0:64], both[:, 64:96]
-    damp = 0.1 * jnp.trace(gram) / NDOCS
-    matrix = gram / NDOCS + damp * jnp.eye(NDOCS, dtype=F32)
-    factor = jnp.linalg.cholesky(matrix)
-    middle = lax.linalg.triangular_solve(factor, cross, left_side=True, lower=True)
-    solved = lax.linalg.triangular_solve(
-        factor, middle, left_side=True, lower=True, transpose_a=True
+    return exchange(
+        inputs[0], out_grads[0], valid, doc_blocks, doc_ids, proj_in, proj_out, test_grads
     )
-    placing = (doc_ids[None, :] == jnp.arange(NDOCS, dtype=jnp.int32)[:, None]).astype(F32)
-    return jnp.dot(placing, solved, precision=HIGH)
 
 
 def solution(mesh):

time: 81.2 us -> 63.1 us (0.78)
  other arithmetic: 12.7 us -> 0 us
  local copies, waits for them, and re-layouts: 7.17 us -> 1.44 us
  Pallas kernels: 59 us -> 61.5 us
  matrix products: 1.25 us -> 0 us
    another operation x5 -> x0, other arithmetic: 12.1 us -> none  [the longest x3 6.52 us: per_device(): factor = jnp.linalg.cholesky(matrix)]
    unnamed x16 -> x0, local copies, waits for them, and re-layouts: 7.09 us -> none
    pallas_call x1, Pallas kernels: 59 us -> 61.5 us  [exchange(): pl.pallas_call(kernel, name='attribution', out_shape=jax.ShapeDtypeStruct...]
    pallas_call x0 -> x1, local copies, waits for them, and re-layouts: none -> 1.44 us  [exchange(): pl.pallas_call(kernel, name='attribution', out_shape=jax.ShapeDtypeStruct...]
    dot_general x1 -> x0, matrix products: 0.82 us -> none  [per_device(): return jnp.dot(placing, solved, precision=HIGH)]
where the time goes in v2:
time: 63.1 us; the launch traced here: 63 us
  Pallas kernels  61.5 us (97%)
  local copies, waits for them, and re-layouts  1.44 us (2%)
    pallas_call x1, Pallas kernels, exchange(): pl.pallas_call(kernel, name='attribution', out_shape=jax.ShapeDtypeStruct...  61.5 us
    pallas_call x1, local copies, waits for them, and re-layouts, exchange(): pl.pallas_call(kernel, name='attribution', out_shape=jax.ShapeDtypeStruct...  1.44 us

profile of v2, /device:TPU:1, one launch (start us, length us, event | category | flops | bytes accessed | tf_op | source)
XLA Modules:
  0.0 63.0 jit_solution(6924157846944433611)
XLA Ops:
  0.0 61.5 %attribution.1 = f32[64,32]{1,0:T(8,128)} custom-call(bf16[128,4096]{1,0:T(8,128)(2,1)} %bitcast.6, bf16[128,14336]{1,0:T(8,128)(2,1)} %bitcast.5, s32[1,128]{1,0:T(1,128)} %valid_hbm.1, s32[1,4]{1,0:T(1,128)} %blocks_hbm.1, bf16[64,128]{1,0:T(8,128)(2,1)} %bitcast.8, bf16[64,448]{1,0:T(8,128)(2,1)} %bitcast.7, bf16[32,4096]{1,0:T(8,128)(2,1)} %test_hbm.1, ...), custom_call_target="tpu_custom_call" | custom-call | tf_op jit(solution)/shard_map/attribution/pallas_call | solution.py:369
  61.5 1.4 %copy.9 = f32[64,32]{0,1:T(8,128)} copy(f32[64,32]{1,0:T(8,128)} %attribution.1) | data formatting | bytes 16384 | tf_op jit(solution)/shard_map/attribution/pallas_call | solution.py:369

commit v3 on v2

v3 whole, which is shorter than its diff:
```python
import jax
import jax.numpy as jnp
from jax import lax
from jax.experimental import pallas as pl
from jax.experimental.pallas import tpu as pltpu
from jax.sharding import PartitionSpec as P

MESH = pl.DeviceIdType.MESH
F32 = jnp.float32
BF16 = jnp.bfloat16
HIGH = lax.Precision.HIGHEST
NX, NY, NZ = 4, 8, 8
NSEQ, NDP = NX * NY, 2 * NZ
KO, KP, KI = 448, 512, 128
NDOCS = 64
NT = (((1,), (1,)), ((), ()))
Y_ORDER = (1, 7, 2, 6, 3, 5, 4)
X_ORDER = (1, 3, 2)


def reach(step, size):
    return min(step, size - step)


PLANE = sorted(
    [(i, j) for i in range(NX) for j in range(NY) if i or j],
    key=lambda o: -reach(o[0], NX) - reach(o[1], NY),
)
STACK = sorted(
    [(k, e) for k in range(NZ) for e in range(2) if k or e],
    key=lambda o: -2 * reach(o[0], NZ) - o[1],
)


def inverse2(p, q, s):
    scale = 1.0 / (p * s - q * q)
    return s * scale, -q * scale, p * scale


def solve(both, ids):
    row = lax.broadcasted_iota(jnp.int32, (NDOCS, 128), 0)
    lane = lax.broadcasted_iota(jnp.int32, (NDOCS, 128), 1)
    diagonal = jnp.where(row == lane, both, 0.0)
    trace = jnp.sum(jnp.sum(diagonal, axis=0, keepdims=True), axis=1, keepdims=True)
    a = jnp.where(lane < NDOCS, both, NDOCS * both) / trace
    a = a + jnp.where(row == lane, 0.1, 0.0)
    for k in range(0, NDOCS, 4):
        r = [a[k + i : k + i + 1, :] for i in range(4)]
        c = [jnp.broadcast_to(a[:, k + i : k + i + 1], (NDOCS, 128)) for i in range(4)]
        m = [[c[j][k + i : k + i + 1] for j in range(4)] for i in range(4)]
        a00, a01, a11 = inverse2(m[0][0], m[1][0], m[1][1])
        b00, b01, b10, b11 = m[2][0], m[3][0], m[2][1], m[3][1]
        w00, w01 = a00 * b00 + a01 * b10, a00 * b01 + a01 * b11
        w10, w11 = a01 * b00 + a11 * b10, a01 * b01 + a11 * b11
        s00 = m[2][2] - (b00 * w00 + b10 * w10)
        s01 = m[3][2] - (b00 * w01 + b10 * w11)
        s11 = m[3][3] - (b01 * w01 + b11 * w11)
        e00, e01, e11 = inverse2(s00, s01, s11)
        t2 = r[2] - (w00 * r[0] + w10 * r[1])
        t3 = r[3] - (w01 * r[0] + w11 * r[1])
        u2, u3 = e00 * t2 + e01 * t3, e01 * t2 + e11 * t3
        u0 = a00 * r[0] + a01 * r[1] - (w00 * u2 + w01 * u3)
        u1 = a01 * r[0] + a11 * r[1] - (w10 * u2 + w11 * u3)
        rest = a - ((c[0] * u0 + c[1] * u1) + (c[2] * u2 + c[3] * u3))
        for i, u in enumerate((u0, u1, u2, u3)):
            rest = jnp.where(row == k + i, u, rest)
        a = rest
    number = lax.broadcasted_iota(jnp.int32, (NDOCS, NDOCS), 0)
    placing = jnp.where(ids == number, 1.0, 0.0)
    return lax.dot_general(
        a[:, 64:96], placing, (((0,), (1,)), ((), ())), precision=HIGH, preferred_element_type=F32
    )


def kernel(
    in_hbm, og_hbm, valid_hbm, blocks_hbm, pin_hbm, pout_hbm, test_hbm, ids_hbm, out_ref,
    tok, grad, valid_ref, blocks_ref, pin_ref, pout_ref, test_ref, ids_ref, w2, w3, pad,
    send_b, recv_b, send_c, recv_c, recv_c2, send_d, recv_d, send_e, recv_e,
    load_sem, gather_send, r2, r2_sib, r3, r3_z, r3_sib, phase_send, phase_recv,
):
    dp = lax.axis_index("dp")
    seq = lax.axis_index("seq")
    z, core = dp // 2, lax.rem(dp, 2)
    x, y = seq // NY, lax.rem(seq, NY)

    def shard(i, j):
        return lax.rem(x + i, NX) * NY + lax.rem(y + j, NY)

    def level(k, e):
        return lax.rem(z + k, NZ) * 2 + (core + e * (1 - 2 * core))

    sibling = (level(0, 1), seq)

    def load(i, src, dst):
        copy = pltpu.make_async_copy(src, dst, load_sem.at[i])
        copy.start()
        return copy

    load_pout = load(0, pout_hbm, pout_ref)
    load_pin = load(1, pin_hbm, pin_ref)
    later = [
        load(2, in_hbm, tok),
        load(3, og_hbm, grad),
        load(4, valid_hbm, valid_ref),
        load(5, blocks_hbm, blocks_ref),
        load(6, test_hbm, test_ref),
        load(7, ids_hbm, ids_ref),
    ]

    barrier = pltpu.get_barrier_semaphore()
    for i, j in PLANE:
        pl.semaphore_signal(barrier, inc=1, device_id=(dp, shard(i, j)), device_id_type=MESH)
    for k, e in STACK:
        pl.semaphore_signal(barrier, inc=1, device_id=(level(k, e), seq), device_id_type=MESH)

    def remote(src, dst, send, recv, target):
        return pltpu.make_async_remote_copy(
            src, dst, send, recv, device_id=target, device_id_type=MESH
        )

    def finish(last):
        for sem, part in (
            (0, w2.at[pl.ds(0, NSEQ - 1), 0]),
            (1, w2.at[pl.ds(0, NSEQ - 1), 0]),
            (2, w3.at[0, 0, pl.ds(0, NSEQ - 1)]),
            (3, w3.at[0, pl.ds(0, 3)]),
            (4, w3.at[0]),
        ):
            remote(part, part, gather_send.at[sem], r2.at[0], sibling).wait_send()
        for phase, buf, count in (
            (0, send_b, NSEQ), (1, recv_c, NDP), (2, recv_c2, NSEQ), (3, recv_d, NSEQ), (4, recv_e, NDP),
        ):
            if phase <= last:
                part = buf.at[pl.ds(0, count - 1)]
                remote(
                    part, part, phase_send.at[phase], phase_recv.at[phase], sibling
                ).wait_send()

    row = lax.broadcasted_iota(jnp.int32, (64, 64), 0)
    col = lax.broadcasted_iota(jnp.int32, (64, 64), 1)
    source = jnp.where(row < 32, 2 * row, 2 * row - 63)
    order = jnp.where(col == source, 1.0, 0.0).astype(BF16)
    pad[...] = jnp.zeros_like(pad)
    load_pout.wait()
    load_pin.wait()
    pad[:, 0:KO] = jnp.dot(order, pout_ref[...], preferred_element_type=F32)
    left = pad[...]
    right = pltpu.roll(left, KP - KO, 1)
    own_out = jnp.where(lax.rem(seq, 2) == 1, right, left).astype(BF16)
    pad[...] = own_out.astype(F32)
    for half in range(2):
        rows = slice(32 * half, 32 * half + 32)
        w2[seq, half, :, 0:256] = own_out[rows, 256:512]
        w2[seq, half, :, 256:384] = pin_ref[rows, :]
    part = lax.rem(z, 4)
    quarter = pad[pl.ds(pl.multiple_of(part * 16, 16), 16), 0:256]
    w3[core, part, seq] = jnp.where(core == 1, quarter[:, 128:256], quarter[:, 0:128]).astype(BF16)

    pl.semaphore_wait(barrier, NSEQ - 1 + NDP - 1)

    def send_2(k, i, j):
        piece = w2.at[k, core]
        remote(piece, piece, gather_send.at[0], r2.at[k], (dp, shard(i, j))).start()

    def recv_2(k):
        piece = w2.at[k, core]
        remote(piece, piece, gather_send.at[0], r2.at[k], sibling).wait_recv()
        remote(piece, piece, gather_send.at[1], r2_sib.at[k], sibling).start()

    def group_of(i):
        return lax.rem(x + i, NX)

    def bundle(tile, quarter_index, group):
        return w3.at[tile, quarter_index, pl.ds(pl.multiple_of(group * NY, NY), NY)]

    def share(group, quarter_index):
        piece = bundle(core, quarter_index, group)
        sem = r3_sib.at[group * 4 + quarter_index]
        remote(piece, piece, gather_send.at[4], sem, sibling).start()

    steps = (1, NZ - 1, 2)

    def lift(i):
        group = group_of(i)
        for j in Y_ORDER + ((0,) if i else ()):
            piece = w3.at[core, part, shard(i, j)]
            remote(piece, piece, gather_send.at[2], r3.at[shard(i, j)], sibling).wait_recv()
        piece = bundle(core, part, group)
        for e, step in enumerate(steps):
            far = step if e < 2 else 2 + 4 * core
            target = (lax.rem(z + far, NZ) * 2 + core, seq)
            sem = r3_z.at[group * 3 + e]
            remote(piece, piece, gather_send.at[3], sem, target).start()
        share(group, part)

    def land(i):
        group = group_of(i)
        for e, step in enumerate(steps):
            far = step if e < 2 else 2 + 4 * core
            origin = lax.rem(z + NZ - far, 4)
            piece = bundle(core, origin, group)
            sem = r3_z.at[group * 3 + e]
            remote(piece, piece, gather_send.at[3], sem, sibling).wait_recv()
            share(group, origin)

    def settle(i):
        group = group_of(i)
        for j in range(NY):
            if i or j:
                k = shard(i, j)
                piece = w2.at[k, 1 - core]
                remote(piece, piece, gather_send.at[1], r2_sib.at[k], sibling).wait_recv()
        for q in range(4):
            piece = bundle(1 - core, q, group)
            sem = r3_sib.at[group * 4 + q]
            remote(piece, piece, gather_send.at[4], sem, sibling).wait_recv()

    for j in Y_ORDER:
        send_2(seq, 0, j)
    for i in X_ORDER:
        send_2(seq, i, 0)
    for i in (0,) + X_ORDER:
        for j in (4, 5, 3, 6, 2, 7, 1) + ((0,) if i else ()):
            piece = w3.at[core, part, seq]
            remote(piece, piece, gather_send.at[2], r3.at[seq], (dp, shard(i, j))).start()

    def pass_on(j):
        k = shard(0, j)
        recv_2(k)
        for i in X_ORDER:
            send_2(k, i, 0)

    def collect(i):
        for j in (0,) + Y_ORDER:
            recv_2(shard(i, j))

    def product(group):
        first = pl.multiple_of(group * NY, NY)
        lane = lax.broadcasted_iota(jnp.int32, (64, 128), 1)
        parts = []
        for q in range(0, NY, 2):
            even, odds = w2[first + q].reshape(64, 384), w2[first + q + 1].reshape(64, 384)
            odd_0 = w3[0, :, first + q + 1].reshape(64, 128)
            joint = jnp.where(lane < 64, even[:, 128:256].astype(F32), odd_0.astype(F32))
            parts += [
                w3[0, :, first + q].reshape(64, 128),
                w3[1, :, first + q].reshape(64, 128),
                even[:, 0:128],
                joint.astype(BF16),
                w3[1, :, first + q + 1].reshape(64, 128),
                odds[:, 0:256],
            ]
        weights = jnp.concatenate(parts, axis=1)
        columns = pl.ds(pl.multiple_of(group * NY * KO, NY * KO), NY * KO)
        pg = lax.dot_general(weights, grad[:, columns], NT, preferred_element_type=F32)
        weights = jnp.concatenate(
            [w2[first + q].reshape(64, 384)[:, 256:384] for q in range(NY)], axis=1
        )
        columns = pl.ds(pl.multiple_of(group * NY * KI, NY * KI), NY * KI)
        px = lax.dot_general(weights, tok[:, columns], NT, preferred_element_type=F32)
        return pg, px

    for j in (1, 7, 2, 6):
        pass_on(j)
    lift(0)
    for j in (3, 5, 4):
        pass_on(j)
    lift(1)
    lift(3)
    for copy in later:
        copy.wait()
    land(0)
    lift(2)
    settle(0)
    pg, px = product(x)
    collect(1)
    land(1)
    collect(3)
    land(3)
    settle(1)
    more_g, more_x = product(group_of(1))
    pg, px = pg + more_g, px + more_x
    settle(3)
    more_g, more_x = product(group_of(3))
    pg, px = pg + more_g, px + more_x
    collect(2)
    land(2)
    settle(2)
    more_g, more_x = product(group_of(2))
    pg, px = pg + more_g, px + more_x

    pg = jnp.where(valid_ref[...] == 1, pg, 0.0)
    block_grad = lax.dot_general(pg, px, NT, precision=HIGH, preferred_element_type=F32)
    folded = jnp.concatenate([block_grad[0:32], block_grad[32:64]], axis=1)
    send_b[...] = folded.reshape(NSEQ, 1, 128)

    def plane_send(phase, src, dst):
        for i, j in PLANE:
            target = (dp, shard(i, j))
            remote(src(shard(i, j)), dst, phase_send.at[phase], phase_recv.at[phase], target).start()

    def stack_send(phase, src, dst):
        for k, e in STACK:
            target = (level(k, e), seq)
            remote(src, dst, phase_send.at[phase], phase_recv.at[phase], target).start()

    def await_all(phase, buf, count):
        part = buf.at[pl.ds(0, count - 1)]
        remote(part, part, phase_send.at[phase], phase_recv.at[phase], sibling).wait_recv()

    plane_send(0, lambda peer: send_b.at[peer], recv_b.at[seq])
    recv_b[seq] = send_b[seq]
    block = lax.broadcasted_iota(jnp.int32, (8, NSEQ), 1)
    doc = lax.broadcasted_iota(jnp.int32, (8, NSEQ), 0)
    owner = jnp.zeros((8, NSEQ), jnp.int32)
    end = 0
    for j in range(4):
        end = end + blocks_ref[0, j]
        owner = owner + jnp.where(block >= end, 1, 0)
    member = jnp.where(owner == doc, 1.0, 0.0)
    await_all(0, recv_b, NSEQ)
    blocks = recv_b[...].reshape(NSEQ, 128)
    docs = jnp.dot(member, blocks, precision=HIGH, preferred_element_type=F32)
    send_c[...] = docs[0:4]
    stack_send(1, send_c, recv_c.at[dp])
    plane_send(2, lambda peer: send_c, recv_c2.at[seq])
    recv_c[dp] = docs[0:4]
    recv_c2[seq] = docs[0:4]

    await_all(1, recv_c, NDP)
    every = recv_c[...].reshape(NDOCS, 128)
    partial = lax.dot_general(docs, every, NT, precision=HIGH, preferred_element_type=F32)
    send_d[...] = partial[0:4]
    plane_send(3, lambda peer: send_d, recv_d.at[seq])
    recv_d[seq] = partial[0:4]

    await_all(2, recv_c2, NSEQ)
    own = jnp.concatenate([recv_c2[t] for t in range(NSEQ)], axis=1)
    high = own.astype(BF16)
    rest = own - high.astype(F32)
    middle = rest.astype(BF16)
    low = (rest - middle.astype(F32)).astype(BF16)
    test = test_ref[...]
    cross = lax.dot_general(high, test, NT, preferred_element_type=F32)
    cross = cross + (
        lax.dot_general(middle, test, NT, preferred_element_type=F32)
        + lax.dot_general(low, test, NT, preferred_element_type=F32)
    )
    send_e[...] = jnp.zeros_like(send_e)
    send_e[:, 64:96] = cross

    await_all(3, recv_d, NSEQ)
    send_e[:, 0:64] = jnp.sum(recv_d[...], axis=0)
    stack_send(4, send_e, recv_e.at[dp])
    recv_e[dp] = send_e[...]
    await_all(4, recv_e, NDP)
    out_ref[...] = solve(recv_e[...].reshape(NDOCS, 128), ids_ref[...])
    finish(4)


def exchange(tokens, outgrad, valid, doc_blocks, doc_ids, proj_in, proj_out, test_grads):
    vmem = pl.BlockSpec(memory_space=pltpu.VMEM)
    dma = pltpu.SemaphoreType.DMA
    return pl.pallas_call(
        kernel,
        name="attribution",
        out_shape=jax.ShapeDtypeStruct((32, NDOCS), F32),
        in_specs=[pl.BlockSpec(memory_space=pltpu.HBM)] * 8,
        out_specs=vmem,
        scratch_shapes=[
            pltpu.VMEM((128, 4096), BF16),
            pltpu.VMEM((128, 14336), BF16),
            pltpu.VMEM((1, 128), jnp.int32),
            pltpu.SMEM((1, 4), jnp.int32),
            pltpu.VMEM((64, KI), BF16),
            pltpu.VMEM((64, KO), BF16),
            pltpu.VMEM((32, 4096), BF16),
            pltpu.VMEM((1, NDOCS), jnp.int32),
            pltpu.VMEM((NSEQ, 2, 32, 384), BF16),
            pltpu.VMEM((2, 4, NSEQ, 16, 128), BF16),
            pltpu.VMEM((64, KP), F32),
            pltpu.VMEM((NSEQ, 1, 128), F32),
            pltpu.VMEM((NSEQ, 1, 128), F32),
            pltpu.VMEM((4, 128), F32),
            pltpu.VMEM((NDP, 4, 128), F32),
            pltpu.VMEM((NSEQ, 4, 128), F32),
            pltpu.VMEM((4, 64), F32),
            pltpu.VMEM((NSEQ, 4, 64), F32),
            pltpu.VMEM((4, 128), F32),
            pltpu.VMEM((NDP, 4, 128), F32),
            dma((8,)),
            dma((5,)),
            dma((NSEQ,)), dma((NSEQ,)), dma((NSEQ,)),
            dma((NX * 3,)), dma((NX * 4,)),
            dma((5,)), dma((5,)),
        ],
        compiler_params=pltpu.CompilerParams(
            collective_id=0, has_side_effects=True, vmem_limit_bytes=60 << 20
        ),
    )(tokens, outgrad, valid, doc_blocks, proj_in.T, proj_out.T, test_grads, doc_ids.reshape(1, NDOCS)).T


def per_device(inputs, out_grads, valid, doc_blocks, doc_ids, proj_in, proj_out, test_grads):
    return exchange(
        inputs[0], out_grads[0], valid, doc_blocks, doc_ids, proj_in, proj_out, test_grads
    )


def solution(mesh):
    in_specs = (
        P("dp", "seq", None),
        P("dp", "seq", None),
        P("dp", "seq"),
        P("dp", None),
        P(),
        P("seq", None),
        P("seq", None),
        P("seq", None),
    )
    return jax.shard_map(
        per_device, mesh=mesh, in_specs=in_specs, out_specs=P(None, "seq"), check_vma=False
    )
```

time: 63.1 us -> 62.8 us (level)
    pallas_call x1 -> x0, local copies, waits for them, and re-layouts: 1.44 us -> none  [exchange(): pl.pallas_call(kernel, name='attribution', out_shape=jax.ShapeDtypeStruct...]
    unnamed x0 -> x1, local copies, waits for them, and re-layouts: none -> 1.32 us
where the time goes in v3:
time: 62.8 us; the launch traced here: 62.6 us
  Pallas kernels  61.3 us (98%)
  local copies, waits for them, and re-layouts  1.32 us (2%)
    pallas_call x1, Pallas kernels, exchange(): pl.pallas_call(kernel, name='attribution', out_shape=jax.ShapeDtypeStruct...  61.3 us
    unnamed x1, local copies, waits for them, and re-layouts  1.32 us

profile of v3, /device:TPU:1, one launch (start us, length us, event | category | flops | bytes accessed | tf_op | source)
XLA Modules:
  0.0 62.6 jit_solution(11229134752326964777)
XLA Ops:
  0.0 61.3 %attribution.1 = f32[32,64]{1,0:T(8,128)} custom-call(bf16[128,4096]{1,0:T(8,128)(2,1)} %bitcast.7, bf16[128,14336]{1,0:T(8,128)(2,1)} %bitcast.6, s32[1,128]{1,0:T(1,128)} %valid_hbm.1, s32[1,4]{1,0:T(1,128)} %blocks_hbm.1, bf16[64,128]{1,0:T(8,128)(2,1)} %bitcast.10, bf16[64,448]{1,0:T(8,128)(2,1)} %bitcast.8, bf16[32,4096]{1,0:T(8,128)(2,1)} %test_hbm.1, ...), custom_call_target="tpu_custom_call" | custom-call | tf_op jit(solution)/shard_map/attribution/pallas_call | solution.py:364
  61.3 1.3 %copy.10 = f32[64,32]{0,1:T(8,128)} copy(f32[64,32]{0,1:T(8,128)} %bitcast.9) | data formatting | bytes 16384

commit v4 on v3

--- a/solution.py
+++ b/solution.py
@@ -37,7 +37,7 @@
     return s * scale, -q * scale, p * scale
 
 
-def solve(both, ids):
+def solve(both):
     row = lax.broadcasted_iota(jnp.int32, (NDOCS, 128), 0)
     lane = lax.broadcasted_iota(jnp.int32, (NDOCS, 128), 1)
     diagonal = jnp.where(row == lane, both, 0.0)
@@ -65,16 +65,12 @@
         for i, u in enumerate((u0, u1, u2, u3)):
             rest = jnp.where(row == k + i, u, rest)
         a = rest
-    number = lax.broadcasted_iota(jnp.int32, (NDOCS, NDOCS), 0)
-    placing = jnp.where(ids == number, 1.0, 0.0)
-    return lax.dot_general(
-        a[:, 64:96], placing, (((0,), (1,)), ((), ())), precision=HIGH, preferred_element_type=F32
-    )
+    return a[:, 64:96]
 
 
 def kernel(
-    in_hbm, og_hbm, valid_hbm, blocks_hbm, pin_hbm, pout_hbm, test_hbm, ids_hbm, out_ref,
-    tok, grad, valid_ref, blocks_ref, pin_ref, pout_ref, test_ref, ids_ref, w2, w3, pad,
+    in_hbm, og_hbm, valid_hbm, blocks_hbm, pin_hbm, pout_hbm, test_hbm, out_ref,
+    tok, grad, valid_ref, blocks_ref, pin_ref, pout_ref, test_ref, w2, w3, pad,
     send_b, recv_b, send_c, recv_c, recv_c2, send_d, recv_d, send_e, recv_e,
     load_sem, gather_send, r2, r2_sib, r3, r3_z, r3_sib, phase_send, phase_recv,
 ):
@@ -104,7 +100,6 @@
         load(4, valid_hbm, valid_ref),
         load(5, blocks_hbm, blocks_ref),
         load(6, test_hbm, test_ref),
-        load(7, ids_hbm, ids_ref),
     ]
 
     barrier = pltpu.get_barrier_semaphore()
@@ -144,14 +139,18 @@
     load_pout.wait()
     load_pin.wait()
     pad[:, 0:KO] = jnp.dot(order, pout_ref[...], preferred_element_type=F32)
-    left = pad[...]
-    right = pltpu.roll(left, KP - KO, 1)
-    own_out = jnp.where(lax.rem(seq, 2) == 1, right, left).astype(BF16)
-    pad[...] = own_out.astype(F32)
+    even_form = pad[...]
+    own_out = jnp.where(lax.rem(seq, 2) == 1, pltpu.roll(even_form, KO, 1), even_form)
+    pad[...] = own_out
+    last = own_out[:, 384:512]
+    last = last + pltpu.roll(last, 64, 1)
+    lane = lax.broadcasted_iota(jnp.int32, (32, 128), 1)
+    folded = jnp.where(lane < 64, last[0:32], last[32:64]).astype(BF16)
     for half in range(2):
         rows = slice(32 * half, 32 * half + 32)
-        w2[seq, half, :, 0:256] = own_out[rows, 256:512]
-        w2[seq, half, :, 256:384] = pin_ref[rows, :]
+        w2[seq, half, 0:2] = own_out[rows, 256:384].astype(BF16).reshape(2, 16, 128)
+        w2[seq, half, 2:4] = pin_ref[rows, :].reshape(2, 16, 128)
+        w2[seq, half, 4] = folded[16 * half : 16 * half + 16]
     part = lax.rem(z, 4)
     quarter = pad[pl.ds(pl.multiple_of(part * 16, 16), 16), 0:256]
     w3[core, part, seq] = jnp.where(core == 1, quarter[:, 128:256], quarter[:, 0:128]).astype(BF16)
@@ -215,14 +214,14 @@
             sem = r3_sib.at[group * 4 + q]
             remote(piece, piece, gather_send.at[4], sem, sibling).wait_recv()
 
+    for i in (0,) + X_ORDER:
+        for j in (4, 5, 3, 6, 2, 7, 1) + ((0,) if i else ()):
+            piece = w3.at[core, part, seq]
+            remote(piece, piece, gather_send.at[2], r3.at[seq], (dp, shard(i, j))).start()
     for j in Y_ORDER:
         send_2(seq, 0, j)
     for i in X_ORDER:
         send_2(seq, i, 0)
-    for i in (0,) + X_ORDER:
-        for j in (4, 5, 3, 6, 2, 7, 1) + ((0,) if i else ()):
-            piece = w3.at[core, part, seq]
-            remote(piece, piece, gather_send.at[2], r3.at[seq], (dp, shard(i, j))).start()
 
     def pass_on(j):
         k = shard(0, j)
@@ -236,58 +235,54 @@
 
     def product(group):
         first = pl.multiple_of(group * NY, NY)
-        lane = lax.broadcasted_iota(jnp.int32, (64, 128), 1)
+
+        def tiles(k):
+            three = [w3[0, :, k], w3[1, :, k], w2[k, :, 0:2]]
+            return [t.reshape(64, 128) for t in three], w2[k, :, 4].reshape(32, 128).astype(F32)
+
         parts = []
         for q in range(0, NY, 2):
-            even, odds = w2[first + q].reshape(64, 384), w2[first + q + 1].reshape(64, 384)
-            odd_0 = w3[0, :, first + q + 1].reshape(64, 128)
-            joint = jnp.where(lane < 64, even[:, 128:256].astype(F32), odd_0.astype(F32))
-            parts += [
-                w3[0, :, first + q].reshape(64, 128),
-                w3[1, :, first + q].reshape(64, 128),
-                even[:, 0:128],
-                joint.astype(BF16),
-                w3[1, :, first + q + 1].reshape(64, 128),
-                odds[:, 0:256],
-            ]
+            (even, last_even), (odd, last_odd) = tiles(first + q), tiles(first + q + 1)
+            upper = jnp.where(lane < 64, last_even, pltpu.roll(last_odd, 64, 1))
+            lower = jnp.where(lane < 64, pltpu.roll(last_even, 64, 1), last_odd)
+            joint = jnp.concatenate([upper, lower], axis=0).astype(BF16)
+            parts += even + [joint] + odd
         weights = jnp.concatenate(parts, axis=1)
         columns = pl.ds(pl.multiple_of(group * NY * KO, NY * KO), NY * KO)
         pg = lax.dot_general(weights, grad[:, columns], NT, preferred_element_type=F32)
         weights = jnp.concatenate(
-            [w2[first + q].reshape(64, 384)[:, 256:384] for q in range(NY)], axis=1
+            [w2[first + q, :, 2:4].reshape(64, 128) for q in range(NY)], axis=1
         )
         columns = pl.ds(pl.multiple_of(group * NY * KI, NY * KI), NY * KI)
         px = lax.dot_general(weights, tok[:, columns], NT, preferred_element_type=F32)
         return pg, px
 
-    for j in (1, 7, 2, 6):
-        pass_on(j)
     lift(0)
-    for j in (3, 5, 4):
-        pass_on(j)
+    pass_on(1)
+    pass_on(7)
     lift(1)
     lift(3)
+    pass_on(2)
+    pass_on(6)
+    lift(2)
+    land(0)
+    pass_on(3)
+    pass_on(5)
+    land(1)
+    pass_on(4)
+    land(3)
+    land(2)
     for copy in later:
         copy.wait()
-    land(0)
-    lift(2)
     settle(0)
     pg, px = product(x)
     collect(1)
-    land(1)
     collect(3)
-    land(3)
-    settle(1)
-    more_g, more_x = product(group_of(1))
-    pg, px = pg + more_g, px + more_x
-    settle(3)
-    more_g, more_x = product(group_of(3))
-    pg, px = pg + more_g, px + more_x
     collect(2)
-    land(2)
-    settle(2)
-    more_g, more_x = product(group_of(2))
-    pg, px = pg + more_g, px + more_x
+    for i in X_ORDER:
+        settle(i)
+        more_g, more_x = product(group_of(i))
+        pg, px = pg + more_g, px + more_x
 
     pg = jnp.where(valid_ref[...] == 1, pg, 0.0)
     block_grad = lax.dot_general(pg, px, NT, precision=HIGH, preferred_element_type=F32)
@@ -354,18 +349,18 @@
     stack_send(4, send_e, recv_e.at[dp])
     recv_e[dp] = send_e[...]
     await_all(4, recv_e, NDP)
-    out_ref[...] = solve(recv_e[...].reshape(NDOCS, 128), ids_ref[...])
+    out_ref[...] = solve(recv_e[...].reshape(NDOCS, 128))
     finish(4)
 
 
-def exchange(tokens, outgrad, valid, doc_blocks, doc_ids, proj_in, proj_out, test_grads):
+def exchange(tokens, outgrad, valid, doc_blocks, proj_in, proj_out, test_grads):
     vmem = pl.BlockSpec(memory_space=pltpu.VMEM)
     dma = pltpu.SemaphoreType.DMA
     return pl.pallas_call(
         kernel,
         name="attribution",
-        out_shape=jax.ShapeDtypeStruct((32, NDOCS), F32),
-        in_specs=[pl.BlockSpec(memory_space=pltpu.HBM)] * 8,
+        out_shape=jax.ShapeDtypeStruct((NDOCS, 32), F32),
+        in_specs=[pl.BlockSpec(memory_space=pltpu.HBM)] * 7,
         out_specs=vmem,
         scratch_shapes=[
             pltpu.VMEM((128, 4096), BF16),
@@ -375,8 +370,7 @@
             pltpu.VMEM((64, KI), BF16),
             pltpu.VMEM((64, KO), BF16),
             pltpu.VMEM((32, 4096), BF16),
-            pltpu.VMEM((1, NDOCS), jnp.int32),
-            pltpu.VMEM((NSEQ, 2, 32, 384), BF16),
+            pltpu.VMEM((NSEQ, 2, 5, 16, 128), BF16),
             pltpu.VMEM((2, 4, NSEQ, 16, 128), BF16),
             pltpu.VMEM((64, KP), F32),
             pltpu.VMEM((NSEQ, 1, 128), F32),
@@ -388,7 +382,7 @@
             pltpu.VMEM((NSEQ, 4, 64), F32),
             pltpu.VMEM((4, 128), F32),
             pltpu.VMEM((NDP, 4, 128), F32),
-            dma((8,)),
+            dma((7,)),
             dma((5,)),
             dma((NSEQ,)), dma((NSEQ,)), dma((NSEQ,)),
             dma((NX * 3,)), dma((NX * 4,)),
@@ -397,13 +391,13 @@
         compiler_params=pltpu.CompilerParams(
             collective_id=0, has_side_effects=True, vmem_limit_bytes=60 << 20
         ),
-    )(tokens, outgrad, valid, doc_blocks, proj_in.T, proj_out.T, test_grads, doc_ids.reshape(1, NDOCS)).T
+    )(tokens, outgrad, valid, doc_blocks, proj_in.T, proj_out.T, test_grads)
 
 
 def per_device(inputs, out_grads, valid, doc_blocks, doc_ids, proj_in, proj_out, test_grads):
-    return exchange(
-        inputs[0], out_grads[0], valid, doc_blocks, doc_ids, proj_in, proj_out, test_grads
-    )
+    solved = exchange(inputs[0], out_grads[0], valid, doc_blocks, proj_in, proj_out, test_grads)
+    placing = (doc_ids[None, :] == jnp.arange(NDOCS, dtype=jnp.int32)[:, None]).astype(F32)
+    return jnp.dot(placing, solved, precision=HIGH)
 
 
 def solution(mesh):

time: 62.8 us -> 60.8 us (0.968)
  Pallas kernels: 61.3 us -> 59.1 us
  matrix products: 0 us -> 1.57 us
  local copies, waits for them, and re-layouts: 1.32 us -> 0.01 us
    pallas_call x1, Pallas kernels: 61.3 us -> 59.1 us  [exchange(): pl.pallas_call(kernel, name='attribution', out_shape=jax.ShapeDtypeStruct...]
    dot_general x0 -> x1, matrix products: none -> 1.57 us  [per_device(): return jnp.dot(placing, solved, precision=HIGH)]
    unnamed x1 -> x2, local copies, waits for them, and re-layouts: 1.32 us -> 0.01 us
where the time goes in v4:
time: 60.8 us; the launch traced here: 60.7 us
  Pallas kernels  59.1 us (97%)
  matrix products  1.57 us (3%)
    pallas_call x1, Pallas kernels, exchange(): pl.pallas_call(kernel, name='attribution', out_shape=jax.ShapeDtypeStruct...  59.1 us
    dot_general x1, matrix products, per_device(): return jnp.dot(placing, solved, precision=HIGH)  1.57 us

profile of v4, /device:TPU:1, one launch (start us, length us, event | category | flops | bytes accessed | tf_op | source)
XLA Modules:
  0.0 60.7 jit_solution(8205227828610599735)
XLA Ops:
  0.0 0.0 copy-start
  0.0 59.1 %attribution.1 = f32[64,32]{1,0:T(8,128)} custom-call(bf16[128,4096]{1,0:T(8,128)(2,1)} %bitcast.6, bf16[128,14336]{1,0:T(8,128)(2,1)} %bitcast.5, s32[1,128]{1,0:T(1,128)} %valid_hbm.1, s32[1,4]{1,0:T(1,128)} %blocks_hbm.1, bf16[64,128]{1,0:T(8,128)(2,1)} %bitcast.8, bf16[64,448]{1,0:T(8,128)(2,1)} %bitcast.7, bf16[32,4096]{1,0:T(8,128)(2,1)} %test_hbm.1), custom_call_target="tpu_custom_call" | custom-call | tf_op jit(solution)/shard_map/attribution/pallas_call | solution.py:359
  59.1 0.0 copy-done
  59.1 1.6 %fusion = f32[64,32]{0,1:T(8,128)} fusion(f32[64,32]{1,0:T(8,128)} %attribution.1, s32[64]{0:T(128)S(1)} %copy-done), kind=kOutput, calls=%fused_computation.1 | convolution fusion | flops 1576960 | bytes 16640 | tf_op jit(solution)/shard_map/dot_general | solution.py:400
Async XLA Ops:
  0.0 59.1 %copy-start = (s32[64]{0:T(128)S(1)}, s32[64]{0:T(128)}, u32[]{:S(2)}) copy-start(s32[64]{0:T(128)} %param.12) | copy-start | bytes 772

commit v5 on v4

--- a/solution.py
+++ b/solution.py
@@ -37,13 +37,12 @@
     return s * scale, -q * scale, p * scale
 
 
-def solve(both):
+def solve(both, ids):
     row = lax.broadcasted_iota(jnp.int32, (NDOCS, 128), 0)
     lane = lax.broadcasted_iota(jnp.int32, (NDOCS, 128), 1)
     diagonal = jnp.where(row == lane, both, 0.0)
     trace = jnp.sum(jnp.sum(diagonal, axis=0, keepdims=True), axis=1, keepdims=True)
-    a = jnp.where(lane < NDOCS, both, NDOCS * both) / trace
-    a = a + jnp.where(row == lane, 0.1, 0.0)
+    a = both / trace + jnp.where(row == lane, 0.1, 0.0)
     for k in range(0, NDOCS, 4):
         r = [a[k + i : k + i + 1, :] for i in range(4)]
         c = [jnp.broadcast_to(a[:, k + i : k + i + 1], (NDOCS, 128)) for i in range(4)]
@@ -65,13 +64,17 @@
         for i, u in enumerate((u0, u1, u2, u3)):
             rest = jnp.where(row == k + i, u, rest)
         a = rest
-    return a[:, 64:96]
+    number = lax.broadcasted_iota(jnp.int32, (NDOCS, NDOCS), 0)
+    placing = jnp.where(ids == number, 1.0, 0.0)
+    return lax.dot_general(
+        a[:, 64:96], placing, (((0,), (1,)), ((), ())), precision=HIGH, preferred_element_type=F32
+    )
 
 
 def kernel(
-    in_hbm, og_hbm, valid_hbm, blocks_hbm, pin_hbm, pout_hbm, test_hbm, out_ref,
-    tok, grad, valid_ref, blocks_ref, pin_ref, pout_ref, test_ref, w2, w3, pad,
-    send_b, recv_b, send_c, recv_c, recv_c2, send_d, recv_d, send_e, recv_e,
+    in_hbm, og_hbm, valid_hbm, blocks_hbm, pin_hbm, pout_hbm, test_hbm, ids_hbm, out_ref,
+    tok, grad, valid_ref, blocks_ref, pin_ref, pout_ref, test_ref, ids_ref, w2, w3, pad,
+    send_b, recv_b, send_c, recv_c, recv_c2, send_d, recv_d, send_e, recv_e, send_f, recv_f,
     load_sem, gather_send, r2, r2_sib, r3, r3_z, r3_sib, phase_send, phase_recv,
 ):
     dp = lax.axis_index("dp")
@@ -100,6 +103,7 @@
         load(4, valid_hbm, valid_ref),
         load(5, blocks_hbm, blocks_ref),
         load(6, test_hbm, test_ref),
+        load(7, ids_hbm, ids_ref),
     ]
 
     barrier = pltpu.get_barrier_semaphore()
@@ -123,7 +127,8 @@
         ):
             remote(part, part, gather_send.at[sem], r2.at[0], sibling).wait_send()
         for phase, buf, count in (
-            (0, send_b, NSEQ), (1, recv_c, NDP), (2, recv_c2, NSEQ), (3, recv_d, NSEQ), (4, recv_e, NDP),
+            (0, send_b, NSEQ), (1, recv_c, NDP), (2, recv_c2, NSEQ), (3, recv_d, NSEQ), (4, recv_e, 8),
+            (5, recv_f, NDP),
         ):
             if phase <= last:
                 part = buf.at[pl.ds(0, count - 1)]
@@ -218,10 +223,10 @@
         for j in (4, 5, 3, 6, 2, 7, 1) + ((0,) if i else ()):
             piece = w3.at[core, part, seq]
             remote(piece, piece, gather_send.at[2], r3.at[seq], (dp, shard(i, j))).start()
+    for i in X_ORDER:
+        send_2(seq, i, 0)
     for j in Y_ORDER:
         send_2(seq, 0, j)
-    for i in X_ORDER:
-        send_2(seq, i, 0)
 
     def pass_on(j):
         k = shard(0, j)
@@ -265,24 +270,30 @@
     pass_on(2)
     pass_on(6)
     lift(2)
-    land(0)
     pass_on(3)
     pass_on(5)
+    pass_on(4)
+    land(0)
     land(1)
-    pass_on(4)
     land(3)
     land(2)
     for copy in later:
         copy.wait()
     settle(0)
     pg, px = product(x)
+    def add(i):
+        more_g, more_x = product(group_of(i))
+        return pg + more_g, px + more_x
+
     collect(1)
     collect(3)
+    settle(1)
+    pg, px = add(1)
     collect(2)
-    for i in X_ORDER:
-        settle(i)
-        more_g, more_x = product(group_of(i))
-        pg, px = pg + more_g, px + more_x
+    settle(3)
+    pg, px = add(3)
+    settle(2)
+    pg, px = add(2)
 
     pg = jnp.where(valid_ref[...] == 1, pg, 0.0)
     block_grad = lax.dot_general(pg, px, NT, precision=HIGH, preferred_element_type=F32)
@@ -305,29 +316,29 @@
 
     plane_send(0, lambda peer: send_b.at[peer], recv_b.at[seq])
     recv_b[seq] = send_b[seq]
-    block = lax.broadcasted_iota(jnp.int32, (8, NSEQ), 1)
-    doc = lax.broadcasted_iota(jnp.int32, (8, NSEQ), 0)
-    owner = jnp.zeros((8, NSEQ), jnp.int32)
+    block = lax.broadcasted_iota(jnp.int32, (NSEQ, 128), 0)
+    owner = jnp.zeros((NSEQ, 128), jnp.int32)
     end = 0
     for j in range(4):
         end = end + blocks_ref[0, j]
         owner = owner + jnp.where(block >= end, 1, 0)
-    member = jnp.where(owner == doc, 1.0, 0.0)
     await_all(0, recv_b, NSEQ)
     blocks = recv_b[...].reshape(NSEQ, 128)
-    docs = jnp.dot(member, blocks, precision=HIGH, preferred_element_type=F32)
-    send_c[...] = docs[0:4]
+    for j in range(4):
+        send_c[j : j + 1] = jnp.sum(jnp.where(owner == j, blocks, 0.0), axis=0, keepdims=True)
     stack_send(1, send_c, recv_c.at[dp])
     plane_send(2, lambda peer: send_c, recv_c2.at[seq])
-    recv_c[dp] = docs[0:4]
-    recv_c2[seq] = docs[0:4]
+    recv_c[dp] = send_c[...]
+    recv_c2[seq] = send_c[...]
 
     await_all(1, recv_c, NDP)
     every = recv_c[...].reshape(NDOCS, 128)
-    partial = lax.dot_general(docs, every, NT, precision=HIGH, preferred_element_type=F32)
-    send_d[...] = partial[0:4]
+    eighth = part * 2 + core
+    mine = recv_c[pl.ds(eighth * 2, 2)].reshape(8, 128)
+    partial = lax.dot_general(mine, every, NT, precision=HIGH, preferred_element_type=F32)
+    send_d[...] = jnp.concatenate([partial[0:4], partial[4:8]], axis=1)
     plane_send(3, lambda peer: send_d, recv_d.at[seq])
-    recv_d[seq] = partial[0:4]
+    recv_d[seq] = send_d[...]
 
     await_all(2, recv_c2, NSEQ)
     own = jnp.concatenate([recv_c2[t] for t in range(NSEQ)], axis=1)
@@ -341,26 +352,38 @@
         lax.dot_general(middle, test, NT, preferred_element_type=F32)
         + lax.dot_general(low, test, NT, preferred_element_type=F32)
     )
-    send_e[...] = jnp.zeros_like(send_e)
-    send_e[:, 64:96] = cross
+    send_f[...] = jnp.zeros_like(send_f)
+    send_f[:, 64:96] = cross
+    stack_send(5, send_f, recv_f.at[dp])
+    recv_f[dp] = send_f[...]
 
     await_all(3, recv_d, NSEQ)
-    send_e[:, 0:64] = jnp.sum(recv_d[...], axis=0)
-    stack_send(4, send_e, recv_e.at[dp])
-    recv_e[dp] = send_e[...]
-    await_all(4, recv_e, NDP)
-    out_ref[...] = solve(recv_e[...].reshape(NDOCS, 128))
-    finish(4)
-
-
-def exchange(tokens, outgrad, valid, doc_blocks, proj_in, proj_out, test_grads):
+    send_e[...] = jnp.sum(recv_d[...], axis=0)
+    for e, step in enumerate(steps):
+        far = step if e < 2 else 2 + 4 * core
+        for other in range(2):
+            target = (lax.rem(z + far, NZ) * 2 + other, seq)
+            remote(send_e, recv_e.at[eighth], phase_send.at[4], phase_recv.at[4], target).start()
+    remote(send_e, recv_e.at[eighth], phase_send.at[4], phase_recv.at[4], sibling).start()
+    recv_e[eighth] = send_e[...]
+    await_all(5, recv_f, NDP)
+    await_all(4, recv_e, 8)
+    gram = recv_e[...]
+    gram = jnp.concatenate([gram, pltpu.roll(gram, 64, 2)], axis=1).reshape(NDOCS, 128)
+    lane = lax.broadcasted_iota(jnp.int32, (NDOCS, 128), 1)
+    both = jnp.where(lane < NDOCS, gram, recv_f[...].reshape(NDOCS, 128))
+    out_ref[...] = solve(both, ids_ref[...])
+    finish(5)
+
+
+def exchange(tokens, outgrad, valid, doc_blocks, doc_ids, proj_in, proj_out, test_grads):
     vmem = pl.BlockSpec(memory_space=pltpu.VMEM)
     dma = pltpu.SemaphoreType.DMA
     return pl.pallas_call(
         kernel,
         name="attribution",
-        out_shape=jax.ShapeDtypeStruct((NDOCS, 32), F32),
-        in_specs=[pl.BlockSpec(memory_space=pltpu.HBM)] * 7,
+        out_shape=jax.ShapeDtypeStruct((32, NDOCS), F32),
+        in_specs=[pl.BlockSpec(memory_space=pltpu.HBM)] * 8,
         out_specs=vmem,
         scratch_shapes=[
             pltpu.VMEM((128, 4096), BF16),
@@ -370,6 +393,7 @@
             pltpu.VMEM((64, KI), BF16),
             pltpu.VMEM((64, KO), BF16),
             pltpu.VMEM((32, 4096), BF16),
+            pltpu.VMEM((1, NDOCS), jnp.int32),
             pltpu.VMEM((NSEQ, 2, 5, 16, 128), BF16),
             pltpu.VMEM((2, 4, NSEQ, 16, 128), BF16),
             pltpu.VMEM((64, KP), F32),
@@ -378,26 +402,29 @@
             pltpu.VMEM((4, 128), F32),
             pltpu.VMEM((NDP, 4, 128), F32),
             pltpu.VMEM((NSEQ, 4, 128), F32),
-            pltpu.VMEM((4, 64), F32),
-            pltpu.VMEM((NSEQ, 4, 64), F32),
+            pltpu.VMEM((4, 128), F32),
+            pltpu.VMEM((NSEQ, 4, 128), F32),
+            pltpu.VMEM((4, 128), F32),
+            pltpu.VMEM((8, 4, 128), F32),
             pltpu.VMEM((4, 128), F32),
             pltpu.VMEM((NDP, 4, 128), F32),
-            dma((7,)),
+            dma((8,)),
             dma((5,)),
             dma((NSEQ,)), dma((NSEQ,)), dma((NSEQ,)),
             dma((NX * 3,)), dma((NX * 4,)),
-            dma((5,)), dma((5,)),
+            dma((6,)), dma((6,)),
         ],
         compiler_params=pltpu.CompilerParams(
             collective_id=0, has_side_effects=True, vmem_limit_bytes=60 << 20
         ),
-    )(tokens, outgrad, valid, doc_blocks, proj_in.T, proj_out.T, test_grads)
+    )(tokens, outgrad, valid, doc_blocks, proj_in.T, proj_out.T, test_grads, doc_ids.reshape(1, NDOCS))
 
 
 def per_device(inputs, out_grads, valid, doc_blocks, doc_ids, proj_in, proj_out, test_grads):
-    solved = exchange(inputs[0], out_grads[0], valid, doc_blocks, proj_in, proj_out, test_grads)
-    placing = (doc_ids[None, :] == jnp.arange(NDOCS, dtype=jnp.int32)[:, None]).astype(F32)
-    return jnp.dot(placing, solved, precision=HIGH)
+    scaled = exchange(
+        inputs[0], out_grads[0], valid, doc_blocks, doc_ids, proj_in, proj_out, test_grads
+    )
+    return NDOCS * scaled.T
 
 
 def solution(mesh):

time: 60.8 us -> 60.3 us (level)
  matrix products: 1.57 us -> 0 us
  other arithmetic: 0 us -> 1.33 us
    dot_general x1 -> x0, matrix products: 1.57 us -> none  [per_device(): return jnp.dot(placing, solved, precision=HIGH)]
    mul x0 -> x1, other arithmetic: none -> 1.33 us  [per_device(): return NDOCS * scaled.T]
where the time goes in v5:
time: 60.3 us; the launch traced here: 60.1 us
  Pallas kernels  58.8 us (98%)
  other arithmetic  1.33 us (2%)
    pallas_call x1, Pallas kernels, exchange(): pl.pallas_call(kernel, name='attribution', out_shape=jax.ShapeDtypeStruct...  58.8 us
    mul x1, other arithmetic, per_device(): return NDOCS * scaled.T  1.33 us

profile of v5, /device:TPU:1, one launch (start us, length us, event | category | flops | bytes accessed | tf_op | source)
XLA Modules:
  0.0 60.1 jit_solution(2458900449386767610)
XLA Ops:
  0.0 58.8 %attribution.1 = f32[32,64]{1,0:T(8,128)} custom-call(bf16[128,4096]{1,0:T(8,128)(2,1)} %bitcast.8, bf16[128,14336]{1,0:T(8,128)(2,1)} %bitcast.7, s32[1,128]{1,0:T(1,128)} %valid_hbm.1, s32[1,4]{1,0:T(1,128)} %blocks_hbm.1, bf16[64,128]{1,0:T(8,128)(2,1)} %bitcast.10, bf16[64,448]{1,0:T(8,128)(2,1)} %bitcast.9, bf16[32,4096]{1,0:T(8,128)(2,1)} %test_hbm.1, ...), custom_call_target="tpu_custom_call" | custom-call | tf_op jit(solution)/shard_map/attribution/pallas_call | solution.py:382
  58.8 1.3 %multiply_bitcast_fusion = f32[64,32]{0,1:T(8,128)} fusion(f32[32,64]{1,0:T(8,128)} %attribution.1), kind=kLoop, calls=%fused_computation | loop fusion | flops 2048 | bytes 16384 | tf_op jit(solution)/shard_map/mul | solution.py:427

commit v6 on v5

--- a/solution.py
+++ b/solution.py
@@ -32,9 +32,32 @@
 )
 
 
-def inverse2(p, q, s):
-    scale = 1.0 / (p * s - q * q)
-    return s * scale, -q * scale, p * scale
+def adjugate4(m):
+    s0 = m[0][0] * m[1][1] - m[1][0] * m[0][1]
+    s1 = m[0][0] * m[1][2] - m[1][0] * m[0][2]
+    s2 = m[0][0] * m[1][3] - m[1][0] * m[0][3]
+    s3 = m[0][1] * m[1][2] - m[1][1] * m[0][2]
+    s4 = m[0][1] * m[1][3] - m[1][1] * m[0][3]
+    s5 = m[0][2] * m[1][3] - m[1][2] * m[0][3]
+    c5 = m[2][2] * m[3][3] - m[3][2] * m[2][3]
+    c4 = m[2][1] * m[3][3] - m[3][1] * m[2][3]
+    c3 = m[2][1] * m[3][2] - m[3][1] * m[2][2]
+    c2 = m[2][0] * m[3][3] - m[3][0] * m[2][3]
+    c1 = m[2][0] * m[3][2] - m[3][0] * m[2][2]
+    c0 = m[2][0] * m[3][1] - m[3][0] * m[2][1]
+    determinant = (s0 * c5 - s1 * c4) + (s2 * c3 + s3 * c2) + (s5 * c0 - s4 * c1)
+    b00 = m[1][1] * c5 - m[1][2] * c4 + m[1][3] * c3
+    b01 = m[0][2] * c4 - m[0][1] * c5 - m[0][3] * c3
+    b02 = m[3][1] * s5 - m[3][2] * s4 + m[3][3] * s3
+    b03 = m[2][2] * s4 - m[2][1] * s5 - m[2][3] * s3
+    b11 = m[0][0] * c5 - m[0][2] * c2 + m[0][3] * c1
+    b12 = m[3][2] * s2 - m[3][0] * s5 - m[3][3] * s1
+    b13 = m[2][0] * s5 - m[2][2] * s2 + m[2][3] * s1
+    b22 = m[3][0] * s4 - m[3][1] * s2 + m[3][3] * s0
+    b23 = m[2][1] * s2 - m[2][0] * s4 - m[2][3] * s0
+    b33 = m[2][0] * s3 - m[2][1] * s1 + m[2][2] * s0
+    rows = [[b00, b01, b02, b03], [b01, b11, b12, b13], [b02, b12, b22, b23], [b03, b13, b23, b33]]
+    return determinant, rows
 
 
 def solve(both, ids):
@@ -47,22 +70,12 @@
         r = [a[k + i : k + i + 1, :] for i in range(4)]
         c = [jnp.broadcast_to(a[:, k + i : k + i + 1], (NDOCS, 128)) for i in range(4)]
         m = [[c[j][k + i : k + i + 1] for j in range(4)] for i in range(4)]
-        a00, a01, a11 = inverse2(m[0][0], m[1][0], m[1][1])
-        b00, b01, b10, b11 = m[2][0], m[3][0], m[2][1], m[3][1]
-        w00, w01 = a00 * b00 + a01 * b10, a00 * b01 + a01 * b11
-        w10, w11 = a01 * b00 + a11 * b10, a01 * b01 + a11 * b11
-        s00 = m[2][2] - (b00 * w00 + b10 * w10)
-        s01 = m[3][2] - (b00 * w01 + b10 * w11)
-        s11 = m[3][3] - (b01 * w01 + b11 * w11)
-        e00, e01, e11 = inverse2(s00, s01, s11)
-        t2 = r[2] - (w00 * r[0] + w10 * r[1])
-        t3 = r[3] - (w01 * r[0] + w11 * r[1])
-        u2, u3 = e00 * t2 + e01 * t3, e01 * t2 + e11 * t3
-        u0 = a00 * r[0] + a01 * r[1] - (w00 * u2 + w01 * u3)
-        u1 = a01 * r[0] + a11 * r[1] - (w10 * u2 + w11 * u3)
-        rest = a - ((c[0] * u0 + c[1] * u1) + (c[2] * u2 + c[3] * u3))
-        for i, u in enumerate((u0, u1, u2, u3)):
-            rest = jnp.where(row == k + i, u, rest)
+        determinant, b = adjugate4(m)
+        scale = 1.0 / determinant
+        u = [(w[0] * r[0] + w[1] * r[1]) + (w[2] * r[2] + w[3] * r[3]) for w in b]
+        rest = a - ((c[0] * u[0] + c[1] * u[1]) + (c[2] * u[2] + c[3] * u[3])) * scale
+        for i in range(4):
+            rest = jnp.where(row == k + i, u[i] * scale, rest)
         a = rest
     number = lax.broadcasted_iota(jnp.int32, (NDOCS, NDOCS), 0)
     placing = jnp.where(ids == number, 1.0, 0.0)
@@ -75,7 +88,7 @@
     in_hbm, og_hbm, valid_hbm, blocks_hbm, pin_hbm, pout_hbm, test_hbm, ids_hbm, out_ref,
     tok, grad, valid_ref, blocks_ref, pin_ref, pout_ref, test_ref, ids_ref, w2, w3, pad,
     send_b, recv_b, send_c, recv_c, recv_c2, send_d, recv_d, send_e, recv_e, send_f, recv_f,
-    load_sem, gather_send, r2, r2_sib, r3, r3_z, r3_sib, phase_send, phase_recv,
+    load_sem, gather_send, r2_row, r2, r2_sib, r3, r3_z, r3_sib, phase_send, phase_recv,
 ):
     dp = lax.axis_index("dp")
     seq = lax.axis_index("seq")
@@ -89,6 +102,12 @@
         return lax.rem(z + k, NZ) * 2 + (core + e * (1 - 2 * core))
 
     sibling = (level(0, 1), seq)
+
+    barrier = pltpu.get_barrier_semaphore()
+    for i, j in PLANE:
+        pl.semaphore_signal(barrier, inc=1, device_id=(dp, shard(i, j)), device_id_type=MESH)
+    for k, e in STACK:
+        pl.semaphore_signal(barrier, inc=1, device_id=(level(k, e), seq), device_id_type=MESH)
 
     def load(i, src, dst):
         copy = pltpu.make_async_copy(src, dst, load_sem.at[i])
@@ -106,12 +125,6 @@
         load(7, ids_hbm, ids_ref),
     ]
 
-    barrier = pltpu.get_barrier_semaphore()
-    for i, j in PLANE:
-        pl.semaphore_signal(barrier, inc=1, device_id=(dp, shard(i, j)), device_id_type=MESH)
-    for k, e in STACK:
-        pl.semaphore_signal(barrier, inc=1, device_id=(level(k, e), seq), device_id_type=MESH)
-
     def remote(src, dst, send, recv, target):
         return pltpu.make_async_remote_copy(
             src, dst, send, recv, device_id=target, device_id_type=MESH
@@ -119,11 +132,12 @@
 
     def finish(last):
         for sem, part in (
-            (0, w2.at[pl.ds(0, NSEQ - 1), 0]),
-            (1, w2.at[pl.ds(0, NSEQ - 1), 0]),
-            (2, w3.at[0, 0, pl.ds(0, NSEQ - 1)]),
-            (3, w3.at[0, pl.ds(0, 3)]),
-            (4, w3.at[0]),
+            (0, w2.at[pl.ds(0, 2), pl.ds(0, 5), 0]),
+            (1, w2.at[pl.ds(0, NX - 1), pl.ds(0, NY - 1), 0]),
+            (2, w2.at[:, :, 0]),
+            (3, w3.at[0, 0, pl.ds(0, NSEQ - 1)]),
+            (4, w3.at[0, pl.ds(0, 3)]),
+            (5, w3.at[0]),
         ):
             remote(part, part, gather_send.at[sem], r2.at[0], sibling).wait_send()
         for phase, buf, count in (
@@ -151,115 +165,109 @@
     last = last + pltpu.roll(last, 64, 1)
     lane = lax.broadcasted_iota(jnp.int32, (32, 128), 1)
     folded = jnp.where(lane < 64, last[0:32], last[32:64]).astype(BF16)
-    for half in range(2):
-        rows = slice(32 * half, 32 * half + 32)
-        w2[seq, half, 0:2] = own_out[rows, 256:384].astype(BF16).reshape(2, 16, 128)
-        w2[seq, half, 2:4] = pin_ref[rows, :].reshape(2, 16, 128)
-        w2[seq, half, 4] = folded[16 * half : 16 * half + 16]
+    third, second = own_out[:, 256:384].astype(BF16), pin_ref[...]
+    w2[x, y, core, 0:2] = jnp.where(core == 1, third[32:64], third[0:32]).reshape(2, 16, 128)
+    w2[x, y, core, 2:4] = jnp.where(core == 1, second[32:64], second[0:32]).reshape(2, 16, 128)
+    w2[x, y, core, 4] = jnp.where(core == 1, folded[16:32], folded[0:16])
     part = lax.rem(z, 4)
     quarter = pad[pl.ds(pl.multiple_of(part * 16, 16), 16), 0:256]
     w3[core, part, seq] = jnp.where(core == 1, quarter[:, 128:256], quarter[:, 0:128]).astype(BF16)
 
     pl.semaphore_wait(barrier, NSEQ - 1 + NDP - 1)
 
-    def send_2(k, i, j):
-        piece = w2.at[k, core]
-        remote(piece, piece, gather_send.at[0], r2.at[k], (dp, shard(i, j))).start()
-
-    def recv_2(k):
-        piece = w2.at[k, core]
-        remote(piece, piece, gather_send.at[0], r2.at[k], sibling).wait_recv()
-        remote(piece, piece, gather_send.at[1], r2_sib.at[k], sibling).start()
+    def column(j):
+        return lax.rem(y + j, NY)
 
     def group_of(i):
         return lax.rem(x + i, NX)
 
-    def bundle(tile, quarter_index, group):
-        return w3.at[tile, quarter_index, pl.ds(pl.multiple_of(group * NY, NY), NY)]
-
-    def share(group, quarter_index):
-        piece = bundle(core, quarter_index, group)
-        sem = r3_sib.at[group * 4 + quarter_index]
-        remote(piece, piece, gather_send.at[4], sem, sibling).start()
+    def pass_on(j):
+        piece = w2.at[x, column(j), core]
+        remote(piece, piece, gather_send.at[1], r2_row.at[column(j)], sibling).wait_recv()
+        for i in X_ORDER:
+            recv = r2.at[column(j)]
+            remote(piece, piece, gather_send.at[1], recv, (dp, shard(i, 0))).start()
+
+    def collect(*steps):
+        for j in steps:
+            three = w2.at[pl.ds(0, NX - 1), column(j), core]
+            remote(three, three, gather_send.at[2], r2.at[column(j)], sibling).wait_recv()
+            four = w2.at[:, column(j), core]
+            remote(four, four, gather_send.at[2], r2_sib.at[column(j)], sibling).start()
+
+    def rows_of(group, count=NY):
+        return pl.ds(pl.multiple_of(group * NY, NY), count)
 
     steps = (1, NZ - 1, 2)
 
     def lift(i):
         group = group_of(i)
-        for j in Y_ORDER + ((0,) if i else ()):
-            piece = w3.at[core, part, shard(i, j)]
-            remote(piece, piece, gather_send.at[2], r3.at[shard(i, j)], sibling).wait_recv()
-        piece = bundle(core, part, group)
+        arrived = w3.at[core, part, rows_of(group, NY if i else NY - 1)]
+        remote(arrived, arrived, gather_send.at[3], r3.at[group], sibling).wait_recv()
+        piece = w3.at[core, part, rows_of(group)]
         for e, step in enumerate(steps):
             far = step if e < 2 else 2 + 4 * core
             target = (lax.rem(z + far, NZ) * 2 + core, seq)
-            sem = r3_z.at[group * 3 + e]
-            remote(piece, piece, gather_send.at[3], sem, target).start()
-        share(group, part)
+            remote(piece, piece, gather_send.at[4], r3_z.at[group], target).start()
 
     def land(i):
         group = group_of(i)
-        for e, step in enumerate(steps):
-            far = step if e < 2 else 2 + 4 * core
-            origin = lax.rem(z + NZ - far, 4)
-            piece = bundle(core, origin, group)
-            sem = r3_z.at[group * 3 + e]
-            remote(piece, piece, gather_send.at[3], sem, sibling).wait_recv()
-            share(group, origin)
-
-    def settle(i):
-        group = group_of(i)
-        for j in range(NY):
-            if i or j:
-                k = shard(i, j)
-                piece = w2.at[k, 1 - core]
-                remote(piece, piece, gather_send.at[1], r2_sib.at[k], sibling).wait_recv()
-        for q in range(4):
-            piece = bundle(1 - core, q, group)
-            sem = r3_sib.at[group * 4 + q]
-            remote(piece, piece, gather_send.at[4], sem, sibling).wait_recv()
+        three = w3.at[core, pl.ds(0, 3), rows_of(group)]
+        remote(three, three, gather_send.at[4], r3_z.at[group], sibling).wait_recv()
+        four = w3.at[core, :, rows_of(group)]
+        remote(four, four, gather_send.at[5], r3_sib.at[group], sibling).start()
+
+    def settle_3():
+        for group in range(NX):
+            four = w3.at[1 - core, :, rows_of(group)]
+            remote(four, four, gather_send.at[5], r3_sib.at[group], sibling).wait_recv()
+
+    def settle(step):
+        pair = lax.rem(y // 2 + step, NY // 2)
+        for q in range(2):
+            four = w2.at[:, 2 * pair + q, 1 - core]
+            remote(four, four, gather_send.at[2], r2_sib.at[2 * pair + q], sibling).wait_recv()
+        return pair
 
     for i in (0,) + X_ORDER:
         for j in (4, 5, 3, 6, 2, 7, 1) + ((0,) if i else ()):
             piece = w3.at[core, part, seq]
-            remote(piece, piece, gather_send.at[2], r3.at[seq], (dp, shard(i, j))).start()
+            remote(piece, piece, gather_send.at[3], r3.at[x], (dp, shard(i, j))).start()
+    own = w2.at[x, y, core]
     for i in X_ORDER:
-        send_2(seq, i, 0)
+        remote(own, own, gather_send.at[0], r2.at[y], (dp, shard(i, 0))).start()
     for j in Y_ORDER:
-        send_2(seq, 0, j)
-
-    def pass_on(j):
-        k = shard(0, j)
-        recv_2(k)
-        for i in X_ORDER:
-            send_2(k, i, 0)
-
-    def collect(i):
-        for j in (0,) + Y_ORDER:
-            recv_2(shard(i, j))
-
-    def product(group):
-        first = pl.multiple_of(group * NY, NY)
-
-        def tiles(k):
-            three = [w3[0, :, k], w3[1, :, k], w2[k, :, 0:2]]
-            return [t.reshape(64, 128) for t in three], w2[k, :, 4].reshape(32, 128).astype(F32)
-
-        parts = []
-        for q in range(0, NY, 2):
-            (even, last_even), (odd, last_odd) = tiles(first + q), tiles(first + q + 1)
+        remote(own, own, gather_send.at[0], r2_row.at[y], (dp, shard(0, j))).start()
+
+    def product(pair):
+        def tiles(i, j):
+            k = i * NY + j
+            three = [w3[0, :, k], w3[1, :, k], w2[i, j, :, 0:2]]
+            return [t.reshape(64, 128) for t in three], w2[i, j, :, 4].reshape(32, 128).astype(F32)
+
+        def columns(ref, width):
+            return jnp.concatenate(
+                [
+                    ref[:, pl.ds(pl.multiple_of((i * NY + 2 * pair) * width, 2 * width), 2 * width)]
+                    for i in range(NX)
+                ],
+                axis=1,
+            )
+
+        parts, parts_in = [], []
+        for i in range(NX):
+            (even, last_even), (odd, last_odd) = tiles(i, 2 * pair), tiles(i, 2 * pair + 1)
             upper = jnp.where(lane < 64, last_even, pltpu.roll(last_odd, 64, 1))
             lower = jnp.where(lane < 64, pltpu.roll(last_even, 64, 1), last_odd)
             joint = jnp.concatenate([upper, lower], axis=0).astype(BF16)
             parts += even + [joint] + odd
-        weights = jnp.concatenate(parts, axis=1)
-        columns = pl.ds(pl.multiple_of(group * NY * KO, NY * KO), NY * KO)
-        pg = lax.dot_general(weights, grad[:, columns], NT, preferred_element_type=F32)
-        weights = jnp.concatenate(
-            [w2[first + q, :, 2:4].reshape(64, 128) for q in range(NY)], axis=1
+            parts_in += [w2[i, 2 * pair + q, :, 2:4].reshape(64, 128) for q in range(2)]
+        pg = lax.dot_general(
+            jnp.concatenate(parts, axis=1), columns(grad, KO), NT, preferred_element_type=F32
         )
-        columns = pl.ds(pl.multiple_of(group * NY * KI, NY * KI), NY * KI)
-        px = lax.dot_general(weights, tok[:, columns], NT, preferred_element_type=F32)
+        px = lax.dot_general(
+            jnp.concatenate(parts_in, axis=1), columns(tok, KI), NT, preferred_element_type=F32
+        )
         return pg, px
 
     lift(0)
@@ -273,26 +281,23 @@
     pass_on(3)
     pass_on(5)
     pass_on(4)
-    land(0)
-    land(1)
-    land(3)
-    land(2)
+    collect(0, 1, 7)
+    for i in (0,) + X_ORDER:
+        land(i)
     for copy in later:
         copy.wait()
-    settle(0)
-    pg, px = product(x)
-    def add(i):
-        more_g, more_x = product(group_of(i))
+    collect(2, 6)
+    settle_3()
+    pg, px = product(settle(0))
+
+    def add(step):
+        more_g, more_x = product(settle(step))
         return pg + more_g, px + more_x
 
-    collect(1)
-    collect(3)
-    settle(1)
+    collect(3, 5)
     pg, px = add(1)
-    collect(2)
-    settle(3)
+    collect(4)
     pg, px = add(3)
-    settle(2)
     pg, px = add(2)
 
     pg = jnp.where(valid_ref[...] == 1, pg, 0.0)
@@ -366,6 +371,7 @@
             remote(send_e, recv_e.at[eighth], phase_send.at[4], phase_recv.at[4], target).start()
     remote(send_e, recv_e.at[eighth], phase_send.at[4], phase_recv.at[4], sibling).start()
     recv_e[eighth] = send_e[...]
+    finish(5)
     await_all(5, recv_f, NDP)
     await_all(4, recv_e, 8)
     gram = recv_e[...]
@@ -373,7 +379,6 @@
     lane = lax.broadcasted_iota(jnp.int32, (NDOCS, 128), 1)
     both = jnp.where(lane < NDOCS, gram, recv_f[...].reshape(NDOCS, 128))
     out_ref[...] = solve(both, ids_ref[...])
-    finish(5)
 
 
 def exchange(tokens, outgrad, valid, doc_blocks, doc_ids, proj_in, proj_out, test_grads):
@@ -394,7 +399,7 @@
             pltpu.VMEM((64, KO), BF16),
             pltpu.VMEM((32, 4096), BF16),
             pltpu.VMEM((1, NDOCS), jnp.int32),
-            pltpu.VMEM((NSEQ, 2, 5, 16, 128), BF16),
+            pltpu.VMEM((NX, NY, 2, 5, 16, 128), BF16),
             pltpu.VMEM((2, 4, NSEQ, 16, 128), BF16),
             pltpu.VMEM((64, KP), F32),
             pltpu.VMEM((NSEQ, 1, 128), F32),
@@ -409,9 +414,9 @@
             pltpu.VMEM((4, 128), F32),
             pltpu.VMEM((NDP, 4, 128), F32),
             dma((8,)),
-            dma((5,)),
-            dma((NSEQ,)), dma((NSEQ,)), dma((NSEQ,)),
-            dma((NX * 3,)), dma((NX * 4,)),
+            dma((6,)),
+            dma((NY,)), dma((NY,)), dma((NY,)),
+            dma((NX,)), dma((NX,)), dma((NX,)),
             dma((6,)), dma((6,)),
         ],
         compiler_params=pltpu.CompilerParams(

time: 60.3 us -> 59.4 us (0.985)
  Pallas kernels: 58.8 us -> 57.9 us
    pallas_call x1, Pallas kernels: 58.8 us -> 57.9 us  [exchange(): pl.pallas_call(kernel, name='attribution', out_shape=jax.ShapeDtypeStruct...]
where the time goes in v6:
time: 59.4 us; the launch traced here: 59.2 us
  Pallas kernels  57.9 us (97%)
  other arithmetic  1.33 us (2%)
    pallas_call x1, Pallas kernels, exchange(): pl.pallas_call(kernel, name='attribution', out_shape=jax.ShapeDtypeStruct...  57.9 us
    mul x1, other arithmetic, per_device(): return NDOCS * scaled.T  1.33 us

profile of v6, /device:TPU:1, one launch (start us, length us, event | category | flops | bytes accessed | tf_op | source)
XLA Modules:
  0.0 59.2 jit_solution(5510357330004400313)
XLA Ops:
  0.0 57.9 %attribution.1 = f32[32,64]{1,0:T(8,128)} custom-call(bf16[128,4096]{1,0:T(8,128)(2,1)} %bitcast.8, bf16[128,14336]{1,0:T(8,128)(2,1)} %bitcast.7, s32[1,128]{1,0:T(1,128)} %valid_hbm.1, s32[1,4]{1,0:T(1,128)} %blocks_hbm.1, bf16[64,128]{1,0:T(8,128)(2,1)} %bitcast.10, bf16[64,448]{1,0:T(8,128)(2,1)} %bitcast.9, bf16[32,4096]{1,0:T(8,128)(2,1)} %test_hbm.1, ...), custom_call_target="tpu_custom_call" | custom-call | tf_op jit(solution)/shard_map/attribution/pallas_call | solution.py:387
  57.9 1.3 %multiply_bitcast_fusion = f32[64,32]{0,1:T(8,128)} fusion(f32[32,64]{1,0:T(8,128)} %attribution.1), kind=kLoop, calls=%fused_computation | loop fusion | flops 2048 | bytes 16384 | tf_op jit(solution)/shard_map/mul | solution.py:432

commit v7 on v6

--- a/solution.py
+++ b/solution.py
@@ -135,9 +135,10 @@
             (0, w2.at[pl.ds(0, 2), pl.ds(0, 5), 0]),
             (1, w2.at[pl.ds(0, NX - 1), pl.ds(0, NY - 1), 0]),
             (2, w2.at[:, :, 0]),
-            (3, w3.at[0, 0, pl.ds(0, NSEQ - 1)]),
-            (4, w3.at[0, pl.ds(0, 3)]),
-            (5, w3.at[0]),
+            (3, w3.at[0, 0, 0, pl.ds(0, NY - 1)]),
+            (4, w3.at[0, 0, pl.ds(0, NX - 1)]),
+            (5, w3.at[0, pl.ds(0, 3)]),
+            (6, w3.at[0]),
         ):
             remote(part, part, gather_send.at[sem], r2.at[0], sibling).wait_send()
         for phase, buf, count in (
@@ -171,15 +172,12 @@
     w2[x, y, core, 4] = jnp.where(core == 1, folded[16:32], folded[0:16])
     part = lax.rem(z, 4)
     quarter = pad[pl.ds(pl.multiple_of(part * 16, 16), 16), 0:256]
-    w3[core, part, seq] = jnp.where(core == 1, quarter[:, 128:256], quarter[:, 0:128]).astype(BF16)
+    w3[core, part, x, y] = jnp.where(core == 1, quarter[:, 128:256], quarter[:, 0:128]).astype(BF16)
 
     pl.semaphore_wait(barrier, NSEQ - 1 + NDP - 1)
 
     def column(j):
         return lax.rem(y + j, NY)
-
-    def group_of(i):
-        return lax.rem(x + i, NX)
 
     def pass_on(j):
         piece = w2.at[x, column(j), core]
@@ -195,44 +193,39 @@
             four = w2.at[:, column(j), core]
             remote(four, four, gather_send.at[2], r2_sib.at[column(j)], sibling).start()
 
-    def rows_of(group, count=NY):
-        return pl.ds(pl.multiple_of(group * NY, NY), count)
-
     steps = (1, NZ - 1, 2)
 
-    def lift(i):
-        group = group_of(i)
-        arrived = w3.at[core, part, rows_of(group, NY if i else NY - 1)]
-        remote(arrived, arrived, gather_send.at[3], r3.at[group], sibling).wait_recv()
-        piece = w3.at[core, part, rows_of(group)]
-        for e, step in enumerate(steps):
-            far = step if e < 2 else 2 + 4 * core
-            target = (lax.rem(z + far, NZ) * 2 + core, seq)
-            remote(piece, piece, gather_send.at[4], r3_z.at[group], target).start()
-
-    def land(i):
-        group = group_of(i)
-        three = w3.at[core, pl.ds(0, 3), rows_of(group)]
-        remote(three, three, gather_send.at[4], r3_z.at[group], sibling).wait_recv()
-        four = w3.at[core, :, rows_of(group)]
-        remote(four, four, gather_send.at[5], r3_sib.at[group], sibling).start()
-
-    def settle_3():
-        for group in range(NX):
-            four = w3.at[1 - core, :, rows_of(group)]
-            remote(four, four, gather_send.at[5], r3_sib.at[group], sibling).wait_recv()
+    def lift(*columns):
+        for j in columns:
+            arrived = w3.at[core, part, pl.ds(0, NX if j else NX - 1), column(j)]
+            remote(arrived, arrived, gather_send.at[4], r3.at[column(j)], sibling).wait_recv()
+            piece = w3.at[core, part, :, column(j)]
+            for e, step in enumerate(steps):
+                far = step if e < 2 else 2 + 4 * core
+                target = (lax.rem(z + far, NZ) * 2 + core, seq)
+                remote(piece, piece, gather_send.at[5], r3_z.at[column(j)], target).start()
+
+    def land(*columns):
+        for j in columns:
+            three = w3.at[core, pl.ds(0, 3), :, column(j)]
+            remote(three, three, gather_send.at[5], r3_z.at[column(j)], sibling).wait_recv()
+            four = w3.at[core, :, :, column(j)]
+            remote(four, four, gather_send.at[6], r3_sib.at[column(j)], sibling).start()
 
     def settle(step):
         pair = lax.rem(y // 2 + step, NY // 2)
         for q in range(2):
+            four = w3.at[1 - core, :, :, 2 * pair + q]
+            remote(four, four, gather_send.at[6], r3_sib.at[2 * pair + q], sibling).wait_recv()
             four = w2.at[:, 2 * pair + q, 1 - core]
             remote(four, four, gather_send.at[2], r2_sib.at[2 * pair + q], sibling).wait_recv()
         return pair
 
-    for i in (0,) + X_ORDER:
-        for j in (4, 5, 3, 6, 2, 7, 1) + ((0,) if i else ()):
-            piece = w3.at[core, part, seq]
-            remote(piece, piece, gather_send.at[3], r3.at[x], (dp, shard(i, j))).start()
+    mine = w3.at[core, part, x, y]
+    for j in (0,) + Y_ORDER:
+        for i in X_ORDER + ((0,) if j else ()):
+            target = (dp, shard(i, j))
+            remote(mine, mine, gather_send.at[4 if i else 3], r3.at[y], target).start()
     own = w2.at[x, y, core]
     for i in X_ORDER:
         remote(own, own, gather_send.at[0], r2.at[y], (dp, shard(i, 0))).start()
@@ -241,8 +234,7 @@
 
     def product(pair):
         def tiles(i, j):
-            k = i * NY + j
-            three = [w3[0, :, k], w3[1, :, k], w2[i, j, :, 0:2]]
+            three = [w3[0, :, i, j], w3[1, :, i, j], w2[i, j, :, 0:2]]
             return [t.reshape(64, 128) for t in three], w2[i, j, :, 4].reshape(32, 128).astype(F32)
 
         def columns(ref, width):
@@ -270,32 +262,32 @@
         )
         return pg, px
 
-    lift(0)
+    lift(0, 1, 7)
     pass_on(1)
     pass_on(7)
-    lift(1)
-    lift(3)
+    lift(2, 6)
     pass_on(2)
     pass_on(6)
-    lift(2)
+    lift(3, 5, 4)
     pass_on(3)
     pass_on(5)
     pass_on(4)
+    land(0, 1, 7)
     collect(0, 1, 7)
-    for i in (0,) + X_ORDER:
-        land(i)
     for copy in later:
         copy.wait()
+    land(2, 6)
     collect(2, 6)
-    settle_3()
     pg, px = product(settle(0))
 
     def add(step):
         more_g, more_x = product(settle(step))
         return pg + more_g, px + more_x
 
+    land(3, 5)
     collect(3, 5)
     pg, px = add(1)
+    land(4)
     collect(4)
     pg, px = add(3)
     pg, px = add(2)
@@ -400,7 +392,7 @@
             pltpu.VMEM((32, 4096), BF16),
             pltpu.VMEM((1, NDOCS), jnp.int32),
             pltpu.VMEM((NX, NY, 2, 5, 16, 128), BF16),
-            pltpu.VMEM((2, 4, NSEQ, 16, 128), BF16),
+            pltpu.VMEM((2, 4, NX, NY, 16, 128), BF16),
             pltpu.VMEM((64, KP), F32),
             pltpu.VMEM((NSEQ, 1, 128), F32),
             pltpu.VMEM((NSEQ, 1, 128), F32),
@@ -414,9 +406,9 @@
             pltpu.VMEM((4, 128), F32),
             pltpu.VMEM((NDP, 4, 128), F32),
             dma((8,)),
-            dma((6,)),
+            dma((7,)),
             dma((NY,)), dma((NY,)), dma((NY,)),
-            dma((NX,)), dma((NX,)), dma((NX,)),
+            dma((NY,)), dma((NY,)), dma((NY,)),
             dma((6,)), dma((6,)),
         ],
         compiler_params=pltpu.CompilerParams(

time: 59.4 us -> 57.8 us (0.973)
  Pallas kernels: 57.9 us -> 56.3 us
    pallas_call x1, Pallas kernels: 57.9 us -> 56.3 us  [exchange(): pl.pallas_call(kernel, name='attribution', out_shape=jax.ShapeDtypeStruct...]
where the time goes in v7:
time: 57.8 us; the launch traced here: 57.6 us
  Pallas kernels  56.3 us (97%)
  other arithmetic  1.33 us (2%)
    pallas_call x1, Pallas kernels, exchange(): pl.pallas_call(kernel, name='attribution', out_shape=jax.ShapeDtypeStruct...  56.3 us
    mul x1, other arithmetic, per_device(): return NDOCS * scaled.T  1.33 us

profile of v7, /device:TPU:1, one launch (start us, length us, event | category | flops | bytes accessed | tf_op | source)
XLA Modules:
  0.0 57.6 jit_solution(12918835758139010819)
XLA Ops:
  0.0 56.3 %attribution.1 = f32[32,64]{1,0:T(8,128)} custom-call(bf16[128,4096]{1,0:T(8,128)(2,1)} %bitcast.8, bf16[128,14336]{1,0:T(8,128)(2,1)} %bitcast.7, s32[1,128]{1,0:T(1,128)} %valid_hbm.1, s32[1,4]{1,0:T(1,128)} %blocks_hbm.1, bf16[64,128]{1,0:T(8,128)(2,1)} %bitcast.10, bf16[64,448]{1,0:T(8,128)(2,1)} %bitcast.9, bf16[32,4096]{1,0:T(8,128)(2,1)} %test_hbm.1, ...), custom_call_target="tpu_custom_call" | custom-call | tf_op jit(solution)/shard_map/attribution/pallas_call | solution.py:379
  56.3 1.3 %multiply_bitcast_fusion = f32[64,32]{0,1:T(8,128)} fusion(f32[32,64]{1,0:T(8,128)} %attribution.1), kind=kLoop, calls=%fused_computation | loop fusion | flops 2048 | bytes 16384 | tf_op jit(solution)/shard_map/mul | solution.py:424

commit v8 on v7

--- a/solution.py
+++ b/solution.py
@@ -30,6 +30,20 @@
     [(k, e) for k in range(NZ) for e in range(2) if k or e],
     key=lambda o: -2 * reach(o[0], NZ) - o[1],
 )
+
+
+def thirds(a):
+    high = a.astype(BF16)
+    rest = a - high.astype(F32)
+    middle = rest.astype(BF16)
+    return high, middle, (rest - middle.astype(F32)).astype(BF16)
+
+
+def product_nt(a, b):
+    (h, m, l), (p, q, r) = thirds(a), thirds(b)
+    left = jnp.concatenate([h, h, m, h, l, m], axis=1)
+    right = jnp.concatenate([p, q, p, r, p, q], axis=1)
+    return lax.dot_general(left, right, NT, preferred_element_type=F32)
 
 
 def adjugate4(m):
@@ -293,7 +307,7 @@
     pg, px = add(2)
 
     pg = jnp.where(valid_ref[...] == 1, pg, 0.0)
-    block_grad = lax.dot_general(pg, px, NT, precision=HIGH, preferred_element_type=F32)
+    block_grad = product_nt(pg, px)
     folded = jnp.concatenate([block_grad[0:32], block_grad[32:64]], axis=1)
     send_b[...] = folded.reshape(NSEQ, 1, 128)
 
@@ -332,7 +346,7 @@
     every = recv_c[...].reshape(NDOCS, 128)
     eighth = part * 2 + core
     mine = recv_c[pl.ds(eighth * 2, 2)].reshape(8, 128)
-    partial = lax.dot_general(mine, every, NT, precision=HIGH, preferred_element_type=F32)
+    partial = product_nt(mine, every)
     send_d[...] = jnp.concatenate([partial[0:4], partial[4:8]], axis=1)
     plane_send(3, lambda peer: send_d, recv_d.at[seq])
     recv_d[seq] = send_d[...]

time: 57.8 us -> 57.6 us (level)
  no operation moved by 1% of the time
where the time goes in v8:
time: 57.6 us; the launch traced here: 57.4 us
  Pallas kernels  56.1 us (97%)
  other arithmetic  1.33 us (2%)
    pallas_call x1, Pallas kernels, exchange(): pl.pallas_call(kernel, name='attribution', out_shape=jax.ShapeDtypeStruct...  56.1 us
    mul x1, other arithmetic, per_device(): return NDOCS * scaled.T  1.33 us

profile of v8, /device:TPU:1, one launch (start us, length us, event | category | flops | bytes accessed | tf_op | source)
XLA Modules:
  0.0 57.4 jit_solution(11374782118852990483)
XLA Ops:
  0.0 56.1 %attribution.1 = f32[32,64]{1,0:T(8,128)} custom-call(bf16[128,4096]{1,0:T(8,128)(2,1)} %bitcast.8, bf16[128,14336]{1,0:T(8,128)(2,1)} %bitcast.7, s32[1,128]{1,0:T(1,128)} %valid_hbm.1, s32[1,4]{1,0:T(1,128)} %blocks_hbm.1, bf16[64,128]{1,0:T(8,128)(2,1)} %bitcast.10, bf16[64,448]{1,0:T(8,128)(2,1)} %bitcast.9, bf16[32,4096]{1,0:T(8,128)(2,1)} %test_hbm.1, ...), custom_call_target="tpu_custom_call" | custom-call | tf_op jit(solution)/shard_map/attribution/pallas_call | solution.py:393
  56.1 1.3 %multiply_bitcast_fusion = f32[64,32]{0,1:T(8,128)} fusion(f32[32,64]{1,0:T(8,128)} %attribution.1), kind=kLoop, calls=%fused_computation | loop fusion | flops 2048 | bytes 16384 | tf_op jit(solution)/shard_map/mul | solution.py:438
